TPU v7x, 256 devices: a whole 4x4x8 slice. The times are simulated.
256 devices in a mesh: seg: 4 (over x), block: 64 (over z, y, core).
Axes of the slice: x: 4, y: 4, z: 8, core: 2. Of those that a mesh axis runs over, the one named last changes fastest.
Arguments:
- jacobian: float32 [1024, 128, 128], P(('seg', 'block')), may hold values from -2 to 2
- implicit_inv: float32 [1024, 128, 128], P(('seg', 'block')), may hold values from -2 to 2, as said below
- input_map: float32 [1024, 128, 64], P(('seg', 'block')), may hold values from -0.75 to 0.75
- controls: float32 [1024, 64], P(('seg', 'block')), may hold values from -2 to 2
- control_step: float32 [1024, 64], P(('seg', 'block')), may hold values from -2 to 2
- state_traj: float32 [1024, 128], P(('seg', 'block')), may hold values from -2 to 2
- terminal: float32 [128], replicated, may hold values from -2 to 2
- init_gap: float32 [128], replicated, may hold values from -3 to 3
- counts: int32 [256], P(('seg', 'block')), may hold values from 2 to 4, as said below
Outputs:
- updated: float32 [1024, 128], P(('seg', 'block'))
- defect_out: float32 [1024, 128], P(('seg', 'block'))
Inputs may be any that keep to these rules, and one draw needn't show every extreme that they name: implicit_inv[k] is the inverse of I - jacobian[k] / 2 + jacobian[k] jacobian[k] / 12. `counts`: some block uses all 4 slots and some only half of 4, rounded down; used slots are the first ones of a block.
All inputs are finite; a program needn't handle non-finite values.
Results may differ from a plain program's by a relative error of at most 0.0003.
Values sent between devices are 32-bit elements; how exact they have to be, the bound alone decides.
No kernel may reach another device: no remote copies, remote signals or barrier semaphores. Data moves between devices by JAX's collectives and lax.ppermute only.
A program may use at most 64 MiB of HBM per device.

v0:
```python
import jax
import jax.numpy as jnp
from jax import lax
from jax.sharding import Mesh
from jax.sharding import PartitionSpec as P

SEG_BLOCK = ("seg", "block_0", "block_1", "block_2")


highest = lax.Precision.HIGHEST


def from_behind(value, axis, by):
    size = lax.axis_size(axis)
    pairs = [(i, i + by) for i in range(size) if 0 <= i + by < size]
    return lax.ppermute(value, axis, pairs)


def neutral_like(value, identity):
    return jax.tree.map(
        lambda a, e: jnp.broadcast_to(jnp.asarray(e, a.dtype), a.shape), value, identity
    )


def gathered_once(value, axis):
    leaves = jax.tree.leaves(value)
    turns = sorted(range(len(leaves)), key=lambda k: -leaves[k].size)
    width = (1, *leaves[turns[0]].shape)[-1]
    lines = [
        jnp.pad(leaves[k].reshape(-1), (0, -leaves[k].size % width)).reshape(-1, width)
        for k in turns
    ]
    both, at, found = (lax.all_gather(jnp.concatenate(lines), axis), 0, {})
    for k, line in zip(turns, lines):
        section = both[:, at : at + len(line)].reshape(len(both), -1)
        found[k] = section[:, : leaves[k].size].reshape(-1, *leaves[k].shape)
        at += len(line)
    numbers = iter(range(len(leaves)))
    return jax.tree.map(lambda _: found[next(numbers)], value)


def prefix_by_axis(value, axes, combine, identity):
    before = start = neutral_like(value, identity)
    total = value
    for axis in reversed(axes):
        size, here = (lax.axis_size(axis), lax.axis_index(axis))
        pieces = gathered_once(total, axis)
        inside, total = (start, start)
        for k in range(size):
            passed = k < here
            total = combine(total, jax.tree.map(lambda part: part[k], pieces))
            inside = jax.tree.map(lambda new, old: jnp.where(passed, new, old), total, inside)
        before = combine(inside, before)
    return before


def batch_matrix(left, right):
    return jnp.einsum("kij,kjl->kil", left, right, precision=highest)


def batch_vector(matrices, vectors):
    return jnp.einsum("kij,kj->ki", matrices, vectors, precision=highest)


def compose(earlier, later):
    return (
        jnp.dot(later[0], earlier[0], precision=highest),
        jnp.dot(later[0], earlier[1], precision=highest) + later[1],
    )


def tree_fold(matrices, vectors):
    while matrices.shape[0] > 1:
        earlier_m = matrices[0::2]
        later_m = matrices[1::2]
        earlier_v = vectors[0::2]
        later_v = vectors[1::2]
        matrices = batch_matrix(later_m, earlier_m)
        vectors = batch_vector(later_m, earlier_v) + later_v
    return (matrices[0], vectors[0])


def body(
    jacobian,
    implicit_inv,
    input_map,
    controls,
    control_step,
    state_traj,
    terminal,
    init_gap,
    counts,
):
    knot_count, state_width = state_traj.shape
    devices = lax.axis_size(SEG_BLOCK)
    position = lax.axis_index(SEG_BLOCK)
    upcoming = from_behind(state_traj[0], SEG_BLOCK, -1)
    upcoming = jnp.where(position == devices - 1, terminal, upcoming)
    slot_ids = jnp.arange(knot_count)
    active = slot_ids < counts[0]
    following = jnp.concatenate([state_traj[1:], upcoming[None]], axis=0)
    next_state = jnp.where((slot_ids + 1 < counts[0])[:, None], following, upcoming[None])
    squared = batch_matrix(jacobian, jacobian)
    identity = jnp.eye(state_width, dtype=jnp.float32)
    explicit = identity + 0.5 * jacobian + squared / 12.0
    implicit_x = (
        next_state
        - 0.5 * batch_vector(jacobian, next_state)
        + batch_vector(squared, next_state) / 12.0
    )
    defect = implicit_x - batch_vector(explicit, state_traj) - batch_vector(input_map, controls)
    transition = batch_matrix(implicit_inv, explicit)
    offset = batch_vector(implicit_inv, batch_vector(input_map, control_step) - defect)
    transition = jnp.where(active[:, None, None], transition, identity[None])
    offset = jnp.where(active[:, None], offset, 0.0)
    neutral = (identity, jnp.zeros((state_width,), jnp.float32))
    element = tree_fold(transition, offset)
    prefix = prefix_by_axis(element, SEG_BLOCK, compose, neutral)
    initial = jnp.dot(prefix[0], init_gap, precision=highest) + prefix[1]

    def advance(current, pieces):
        step_matrix, step_offset = pieces
        fresh_state = jnp.dot(step_matrix, current, precision=highest) + step_offset
        return (fresh_state, fresh_state)

    _, corrections = lax.scan(advance, initial, (transition, offset))
    updated = jnp.where(active[:, None], next_state + corrections, 0.0)
    defect_out = jnp.where(active[:, None], defect, 0.0)
    return (updated, defect_out)


def solution(mesh):
    split = Mesh(
        mesh.devices.reshape(mesh.shape["seg"], 8, 4, 2), ("seg", "block_0", "block_1", "block_2")
    )
    in_specs = (
        P(SEG_BLOCK, None, None),
        P(SEG_BLOCK, None, None),
        P(SEG_BLOCK, None, None),
        P(SEG_BLOCK, None),
        P(SEG_BLOCK, None),
        P(SEG_BLOCK, None),
        P(),
        P(),
        P(SEG_BLOCK),
    )
    out_specs = (P(SEG_BLOCK, None), P(SEG_BLOCK, None))
    return jax.shard_map(body, mesh=split, in_specs=in_specs, out_specs=out_specs, check_vma=False)
```

profile of v0, /device:TPU:2, one launch (start us, length us, event | category | flops | bytes accessed | tf_op | source)
XLA Modules:
  0.0 85.0 jit_solution(15264869625999670605)
XLA Ops:
  0.6 0.7 slice_bitcast_fusion.77
  1.4 9.6 %collective-permute-start = (f32[128]{0:T(128)S(1)}, f32[128]{0:T(128)S(1)}, u32[]{:S(2)}, u32[]{:S(2)}) collective-permute-start(f32[128]{0:T(128)S(1)} %slice_bitcast_fusion.77), channel_id=1, source_target_pairs={{1,0},{2,1},{3,2},{4,3},{5,4},{6,5},{7,6},{8,7},{9,8},{10,9},{11,1... | collective-permute-start | bytes 1544 | tf_op jit(solution)/shard_map/ppermute | solution.py:16
  11.0 0.7 copy-done.3
  12.4 1.5 %fusion.129 = f32[4,128,128]{2,1,0:T(8,128)S(1)} fusion(f32[4,128,128]{2,1,0:T(8,128)} %param.11), kind=kOutput, calls=%fused_computation.224 | convolution fusion | flops 100663296 | bytes 524288 | tf_op jit(solution)/shard_map/kij,kjl->kil/dot_general | solution.py:58
  13.9 0.4 fusion.5
  14.3 0.3 fusion.30
  14.6 0.6 copy-done.2
  15.4 0.5 copy-done.5
  16.1 0.5 fusion.35
  16.9 0.6 copy-done.7
  17.6 0.5 fusion.132
  18.1 0.5 fusion.131
  18.7 0.7 broadcast_select_fusion
  19.3 0.5 fusion.134
  20.0 0.3 fusion.32
  20.6 1.9 %all-gather.4 = f32[2,129,128]{2,1,0:T(8,128)S(1)} all-gather(f32[1,129,128]{2,1,0:T(8,128)S(1)} %maximum_bitcast_fusion), channel_id=2, replica_groups=mesh['seg'=4,'block_0'=8,'block_1'=4,'block_2'=2] {'block_2'}, dimensions={0}, use_global_device_ids=true | all-gather | bytes 198144 | tf_op jit(solution)/shard_map/all_gather | solution.py:33
  22.8 0.2 fusion.61
  23.3 12.4 %all-gather.5 = f32[4,129,128]{2,1,0:T(8,128)S(1)} all-gather(f32[1,129,128]{2,1,0:T(8,128)S(1)} %maximum_bitcast_fusion.1), channel_id=3, replica_groups=mesh['seg'=4,'block_0'=8,'block_1'=4,'block_2'=2] {'block_1'}, dimensions={0}, use_global_device_ids=true | all-gather | bytes 330240 | tf_op jit(solution)/shard_map/all_gather | solution.py:33
  35.9 0.2 fusion.58
  36.8 0.2 fusion.64
  37.8 0.3 fusion.42
  38.1 25.6 %all-gather.6 = f32[8,129,128]{2,1,0:T(8,128)S(1)} all-gather(f32[1,129,128]{2,1,0:T(8,128)S(1)} %maximum_bitcast_fusion.2), channel_id=4, replica_groups=mesh['seg'=4,'block_0'=8,'block_1'=4,'block_2'=2] {'block_0'}, dimensions={0}, use_global_device_ids=true | all-gather | bytes 594432 | tf_op jit(solution)/shard_map/all_gather | solution.py:33
  63.9 0.2 fusion.57
  65.7 0.3 fusion.71
  67.2 12.6 %all-gather.7 = f32[4,129,128]{2,1,0:T(8,128)S(1)} all-gather(f32[1,129,128]{2,1,0:T(8,128)S(1)} %maximum_bitcast_fusion.3), channel_id=5, replica_groups=mesh['seg'=4,'block_0'=8,'block_1'=4,'block_2'=2] {'seg'}, dimensions={0}, use_global_device_ids=true | all-gather | bytes 330240 | tf_op jit(solution)/shard_map/all_gather | solution.py:33
  80.0 0.2 fusion.56
  80.4 0.3 fusion.51
  81.3 0.3 fusion.73
  82.0 0.2 convolution_select_fusion
  82.6 0.5 copy-done.6
  83.3 1.1 %while.13 = (s32[]{:T(128)}, f32[128]{0:T(128)S(1)}, f32[4,128]{1,0:T(4,128)S(1)}, f32[4,128,128]{2,1,0:T(8,128)S(1)}, f32[4,128]{1,0:T(4,128)S(1)}) while((s32[]{:T(128)}, f32[128]{0:T(128)S(1)}, f32[4,128]{1,0:T(4,128)S(1)}, f32[4,128,128]{2,1,0:T(8,128)S(1)}, f32[4,128]{1,0:T(4,128)S(1)}) %tuple.27), condition=%wide.region_1.2_spmd.clone, body=%wide.region_0.1_spmd.sunk.clone | while | flops 196738 | bytes 70217 | solution.py:126
  84.4 0.7 add_select_fusion
  (78 shorter events, 9.2 us)
Async XLA Ops:
  0.6 13.2 %copy-start = (f32[4,128,128]{2,1,0:T(8,128)S(1)}, f32[4,128,128]{2,1,0:T(8,128)}, u32[]{:S(2)}) copy-start(f32[4,128,128]{2,1,0:T(8,128)} %param.12) | copy-start | bytes 786436
  1.4 15.5 %collective-permute-start = (f32[128]{0:T(128)S(1)}, f32[128]{0:T(128)S(1)}, u32[]{:S(2)}, u32[]{:S(2)}) collective-permute-start(f32[128]{0:T(128)S(1)} %slice_bitcast_fusion.77), channel_id=1, source_target_pairs={{1,0},{2,1},{3,2},{4,3},{5,4},{6,5},{7,6},{8,7},{9,8},{10,9},{11,1... | collective-permute-start | bytes 1544 | tf_op jit(solution)/shard_map/ppermute | solution.py:16
  11.0 0.7 copy-start.3
  12.4 1.5 %copy-start.1 = (f32[4,128,128]{2,1,0:T(8,128)S(1)}, f32[4,128,128]{2,1,0:T(8,128)}, u32[]{:S(2)}) copy-start(f32[4,128,128]{2,1,0:T(8,128)} %param.11) | copy-start | bytes 786436
  14.3 0.9 %copy-start.2 = (f32[4,128,64]{1,2,0:T(8,128)S(1)}, f32[4,128,64]{1,2,0:T(8,128)}, u32[]{:S(2)}) copy-start(f32[4,128,64]{1,2,0:T(8,128)} %param.13) | copy-start | bytes 393220
  14.3 0.9 %copy-start.4 = (f32[4,64]{1,0:T(4,128)S(1)}, f32[4,64]{1,0:T(4,128)}, u32[]{:S(2)}) copy-start(f32[4,64]{1,0:T(4,128)} %param.15) | copy-start | bytes 3076
  15.2 0.7 copy-start.5
  16.9 0.7 copy-start.7
  82.4 0.7 copy-start.6
where the time goes:
time: 85.3 us; the launch traced here: 85 us
  blocking collectives  52.6 us (62%)
  matrix products  15.5 us (18%)
  starting transfers between devices  9.61 us (11%)
  local copies, waits for them, and re-layouts  3.94 us (5%)
  between operations  1.68 us (2%)
  other arithmetic  1.62 us (2%)
    all_gather x4, blocking collectives, gathered_once(): both, at, found = (lax.all_gather(jnp.concatenate(lines), axis), 0, {})  52.6 us
    ppermute x1, starting transfers between devices, from_behind(): return lax.ppermute(value, axis, pairs)  9.61 us
    dot_general x22, matrix products, compose(): jnp.dot(later[0], earlier[0], precision=highest)  4.89 us
    dot_general x22, matrix products, compose(): jnp.dot(later[0], earlier[1], precision=highest) + later[1]  4.3 us
    dot_general x8, matrix products, batch_vector(): return jnp.einsum('kij,kj->ki', matrices, vectors, precision=highest)  3.03 us
    unnamed x16, local copies, waits for them, and re-layouts  2.88 us
    dot_general x4, matrix products, batch_matrix(): return jnp.einsum('kij,kjl->kil', left, right, precision=highest)  2.37 us
  transfers between devices with their start and end apart: 1, of which 0 were waited for; matrix products, arithmetic and copies ran while one was open for 4% of the time, Pallas kernels for 0%

commit v1 on v0

v1 whole, which is shorter than its diff:
```python
import functools

import jax
import jax.numpy as jnp
from jax import lax
from jax.experimental import pallas as pl
from jax.experimental.pallas import tpu as pltpu
from jax.sharding import Mesh
from jax.sharding import PartitionSpec as P

AXES = ("seg", "z", "y", "core")
ROWS = 136


NN = (((1,), (0,)), ((), ()))
NT = (((1,), (1,)), ((), ()))


def parts(value, count=2):
    pieces = []
    for _ in range(count):
        piece = value.astype(jnp.bfloat16)
        pieces.append(piece)
        value = value - piece.astype(jnp.float32)
    return pieces


def product(left, right, dims=NN):
    pairs = [(i, j) for i in range(len(left)) for j in range(len(left) - i)]
    pairs = pairs[::-1]
    (left_axis,), (right_axis,) = dims[0]
    return lax.dot_general(
        jnp.concatenate([left[i] for i, _ in pairs], axis=left_axis),
        jnp.concatenate([right[j] for _, j in pairs], axis=right_axis),
        dims,
        preferred_element_type=jnp.float32,
    )


exact = functools.partial(parts, count=3)


def rows_of(shape):
    return lax.broadcasted_iota(jnp.int32, shape, 0)


def eye_of(shape):
    return jnp.where(rows_of(shape) == lax.broadcasted_iota(jnp.int32, shape, 1), 1.0, 0.0)


def compose(earlier, later):
    width = earlier.shape[1]
    out = product(parts(earlier), parts(later[:width]))
    row = rows_of(out.shape)
    return jnp.where(row < width, out, jnp.where(row == width, out + later, earlier))


def maps_kernel(
    counts, jacobian, inverse, input_map, controls, control_step, states, gap, total, partial
):
    knots, width = states.shape
    first = jnp.bool_(True)
    for name in AXES:
        first = jnp.logical_and(first, lax.axis_index(name) == 0)
    start = jnp.where(first, gap[...] + states[0:1, :], 0.0)
    row = rows_of((ROWS, width))
    eye = eye_of((ROWS, width))
    drive = exact(controls[...] + control_step[...])
    running = None
    for k in range(knots):
        pushed = product(drive, exact(input_map[k]))
        left = jnp.concatenate(
            [jacobian[k].T, jnp.broadcast_to(pushed[k : k + 1], (ROWS - width, width))], axis=0
        )
        step = product(exact(left), exact(inverse[k]), NT) + eye
        step = jnp.where(k < counts[0], step, eye)
        matrix = exact(step[:width])
        if k == 0:
            moved = product(exact(jnp.broadcast_to(start, (8, width))), matrix)
            running = step + jnp.where(row >= width, jnp.broadcast_to(moved[0:1], step.shape), 0.0)
        else:
            running = product(exact(running), matrix) + jnp.where(row >= width, step, 0.0)
        partial[k] = running
    total[...] = jnp.where(row == width + 1, jnp.broadcast_to(states[0:1, :], running.shape), running)


def defect_kernel(counts, jacobian, input_map, controls, states, base, last):
    knots, width = states.shape
    count = counts[0]
    slot = rows_of((knots, width))
    here = states[...]
    following = jnp.concatenate([here[1:], jnp.zeros((1, width), jnp.float32)], axis=0)
    following = jnp.where(slot + 1 < count, following, 0.0)
    plus = following + here
    minus = following - here
    both = parts(jnp.concatenate([plus, minus], axis=0))
    forces = parts(controls[...])
    rows = []
    for k in range(knots):
        matrix = parts(jacobian[k])
        once = product(both, matrix, NT)
        twice = product(parts(once), matrix, NT)
        forced = product(forces, parts(input_map[k]))
        rows.append(
            minus[k : k + 1]
            - 0.5 * once[k : k + 1]
            + twice[knots + k : knots + k + 1] / 12.0
            - forced[k : k + 1]
        )
    base[...] = jnp.where(slot < count, jnp.concatenate(rows, axis=0), 0.0)
    last[...] = jacobian[count - 1]


def pair_kernel(axis, own, other, total):
    odd = lax.axis_index(axis) % 2 == 1
    mine, theirs = own[...], other[...]
    total[...] = compose(jnp.where(odd, theirs, mine), jnp.where(odd, mine, theirs))


def choose(pair):
    if pair[0] is pair[1]:
        return pair[0][...]
    return jnp.where(lax.axis_index("core") == 0, pair[0][...], pair[1][...])


def four_kernel(axis, shift, own, *refs):
    near, far, cross = refs[0:2], refs[2:4], refs[4:6]
    total, beside, others = refs[6:]
    place = lax.axis_index(axis) >> shift
    odd = place % 2 == 1
    high = place >= 2
    a, b, c, d = own[...], choose(near), choose(far), choose(cross)
    beside[...] = b
    mine = compose(jnp.where(odd, b, a), jnp.where(odd, a, b))
    rest = compose(jnp.where(odd, d, c), jnp.where(odd, c, d))
    others[...] = rest
    total[...] = compose(jnp.where(high, rest, mine), jnp.where(high, mine, rest))


def before_kernel(levels, *refs):
    out = refs[-1]
    neutral = eye_of(out.shape)
    before = None
    for (axis, bit), ref in zip(levels, refs):
        present = (lax.axis_index(axis) >> bit) % 2 == 1
        chosen = jnp.where(present, ref[...], neutral)
        before = chosen if before is None else compose(chosen, before)
    out[...] = before


def reach_kernel(before, partial, reach):
    width = before.shape[1]
    row = rows_of(before.shape)
    left = parts(before[...])
    for k in range(partial.shape[0]):
        reach[k] = product(left, parts(partial[k, :width])) + jnp.where(row == width, partial[k], 0.0)


def final_kernel(
    counts, near_a, near_b, far_a, far_b, cross, reach, upcoming, base, last, updated, defect
):
    knots, width = base.shape
    near, far = choose((near_a, near_b)), choose((far_a, far_b))
    x = lax.axis_index("seg")
    count = counts[0]
    slot = rows_of((knots, width))
    start = jnp.where(
        x == 3,
        cross[width : width + 1],
        jnp.where(x == 2, far[width : width + 1], jnp.where(x == 1, near[width : width + 1], 0.0)),
    )

    def wide(row):
        return jnp.broadcast_to(row, (8, width))

    second = jnp.where(x == 3, far, cross[...])
    moved = product(parts(wide(start)), parts(second[:width]))[0:1] + second[width : width + 1]
    start = jnp.where(x >= 2, moved, start)
    moved = product(parts(wide(start)), parts(near[:width]))[0:1] + near[width : width + 1]
    start = parts(wide(jnp.where(x == 3, moved, start)))
    for k in range(knots):
        state = product(start, parts(reach[k, :width]))[0:1] + reach[k, width : width + 1]
        updated[k : k + 1] = jnp.where(k < count, state, 0.0)
    settled = jnp.logical_not(
        jnp.logical_and(
            lax.axis_index("z") == lax.axis_size("z") - 1,
            jnp.logical_and(lax.axis_index("y") == 3, lax.axis_index("core") == 1),
        )
    )
    lead = width + 1
    after = jnp.where(x == 1, cross[lead : lead + 1], near[lead : lead + 1])
    after = jnp.where(jnp.logical_or(settled, x == 3), upcoming[...], after)
    matrix = parts(last[...])
    once = product(parts(wide(after)), matrix, NT)
    twice = product(parts(once), matrix, NT)
    met = after - 0.5 * once[0:1] + twice[0:1] / 12.0
    defect[...] = base[...] + jnp.where(slot == count - 1, jnp.broadcast_to(met, slot.shape), 0.0)


def swap(value, axis, partner):
    return lax.ppermute(value, axis, [(i, partner(i)) for i in range(lax.axis_size(axis))])


SMEM = pl.BlockSpec(memory_space=pltpu.SMEM)
VMEM = pl.BlockSpec(memory_space=pltpu.VMEM)


def call(kernel, out, operands, scalars=0, local=True, held=(), flops=0):
    operands = [
        pltpu.with_memory_space_constraint(value, pltpu.VMEM) if k in held else value
        for k, value in enumerate(operands)
    ]
    single = not isinstance(out, list)
    shapes = [out] if single else out
    make = pltpu.VMEM if local else jax.ShapeDtypeStruct
    shapes = tuple(make(shape, jnp.float32) for shape in shapes)
    result = pl.pallas_call(
        kernel,
        out_shape=shapes,
        in_specs=[SMEM] * scalars + [VMEM] * (len(operands) - scalars),
        out_specs=tuple(VMEM for _ in shapes),
        cost_estimate=pl.CostEstimate(flops=flops, bytes_accessed=400_000, transcendentals=0),
    )(*operands)
    return result[0] if single else result


def body(jacobian, inverse, input_map, controls, control_step, states, terminal, gap, counts):
    knots, width = states.shape
    z, _, core = (lax.axis_index(name) for name in AXES[1:])
    square = (ROWS, width)
    input_map = jnp.swapaxes(input_map, 1, 2)
    total, partial = call(
        maps_kernel,
        [square, (knots, *square)],
        (counts, jacobian, inverse, input_map, controls, control_step, states, gap[None]),
        scalars=1,
    )
    base, last = call(
        defect_kernel,
        [(knots, width), (width, width)],
        (counts, jacobian, input_map, controls, states),
        scalars=1,
        held=range(1, 5),
    )

    def lead(pieces):
        return pieces[width + 1 : width + 2]

    def apart(value, axis, partners):
        size = lax.axis_size(axis)
        pairs = [(i * 2 + c, partners[c](i) * 2 + c) for i in range(size) for c in range(2)]
        return lax.ppermute(value, (axis, "core"), pairs)

    def across(value):
        return swap(value, "core", lambda i: i ^ 1)

    levels = [("core", 0)]
    other = across(total)
    earlier = [other]
    upcoming = lead(other)
    settled = core == 0
    total = call(functools.partial(pair_kernel, "core"), square, (total, other), held=(0, 1))

    def gathered(total, axis, masks, shared, first):
        def both():
            return swap(total, axis, lambda i: i ^ shared)

        def each():
            return apart(total, axis, [lambda i, d=d: i ^ d for d in masks])

        if first:
            common, own = both(), each()
        else:
            own, common = each(), both()
        passed = across(own)
        return {shared: (common, common), masks[0]: (own, passed), masks[1]: (passed, own)}

    def one(arrival):
        return jnp.where(core == 0, lead(arrival[0]), lead(arrival[1]))

    def four(total, upcoming, settled, axis, shift, arrivals):
        place = lax.axis_index(axis) >> shift
        operands = [total]
        for arrival in arrivals:
            operands.extend(arrival)
        whole, near, others = call(
            functools.partial(four_kernel, axis, shift), [square, square, square], operands, held=range(7)
        )
        after = jnp.where(place % 2 == 1, one(arrivals[2]), one(arrivals[0]))
        upcoming = jnp.where(settled, upcoming, after)
        settled = jnp.logical_or(settled, place < 3)
        levels.extend([(axis, shift), (axis, shift + 1)])
        earlier.extend([near, others])
        return whole, upcoming, settled

    found = gathered(total, "y", (2, 1), 3, False)
    total, upcoming, settled = four(total, upcoming, settled, "y", 0, [found[1], found[2], found[3]])
    levels.append(("z", 0))
    other = swap(total, "z", lambda i: i ^ 1)
    earlier.append(other)
    upcoming = jnp.where(settled, upcoming, lead(other))
    settled = jnp.logical_or(settled, z % 2 == 0)
    total = call(functools.partial(pair_kernel, "z"), square, (total, other), held=(0, 1))
    found = gathered(total, "z", (6, 5), 2, True)
    total, upcoming, settled = four(total, upcoming, settled, "z", 1, [found[2], found[5], found[6]])
    upcoming = jnp.where(jnp.logical_and(~settled, lax.axis_index("seg") == 3), terminal[None], upcoming)
    found = gathered(total, "seg", (2, 1), 3, False)
    before = call(functools.partial(before_kernel, levels), square, earlier, held=range(len(earlier)))
    reach = call(reach_kernel, (knots, *square), (before, partial), held=(0, 1))
    updated, defect = call(
        final_kernel,
        [(knots, width), (knots, width)],
        (counts, *found[1], *found[2], *found[3][:1], reach, upcoming, base, last),
        scalars=1,
        local=False,
        held=range(1, 10),
    )
    return updated, defect


def solution(mesh):
    split = Mesh(mesh.devices.reshape(mesh.shape["seg"], 8, 4, 2), AXES)
    in_specs = (
        P(AXES, None, None),
        P(AXES, None, None),
        P(AXES, None, None),
        P(AXES, None),
        P(AXES, None),
        P(AXES, None),
        P(),
        P(),
        P(AXES),
    )
    out_specs = (P(AXES, None), P(AXES, None))
    return jax.shard_map(body, mesh=split, in_specs=in_specs, out_specs=out_specs, check_vma=False)
```

time: 85.3 us -> 42.5 us (0.50)
  blocking collectives: 52.6 us -> 0 us
  waiting for transfers between devices: 0.01 us -> 15.7 us
  matrix products: 15.5 us -> 0 us
  Pallas kernels: 0 us -> 7.48 us
  starting transfers between devices: 9.61 us -> 16.5 us
  local copies, waits for them, and re-layouts: 3.94 us -> 0.7 us
  other arithmetic: 1.62 us -> 0.01 us
    all_gather x4 -> x0, blocking collectives: 52.6 us -> none  [gathered_once(): both, at, found = (lax.all_gather(jnp.concatenate(lines), axis), 0, {})]
    ppermute x1 -> x11, waiting for transfers between devices: 0.01 us -> 15.7 us  [the longest x8 10.6 us: swap(): lax.ppermute(value, axis, [(i, partner(i)) for i in range(lax.axis_size(a...]
    dot_general x61 -> x0, matrix products: 15.5 us -> none  [the longest x22 4.89 us: compose(): jnp.dot(later[0], earlier[0], precision=highest)]
    pallas_call x0 -> x9, Pallas kernels: none -> 7.48 us  [call(): pl.pallas_call(kernel, out_shape=shapes, in_specs=[SMEM] * scalars + [VME...]
    ppermute x1 -> x11, starting transfers between devices: 9.61 us -> 16.5 us  [the longest x3 11.9 us: apart(): return lax.ppermute(value, (axis, 'core'), pairs)]
    unnamed x16 -> x10, local copies, waits for them, and re-layouts: 2.88 us -> 0.7 us
    select_n x5 -> x1, other arithmetic: 1.48 us -> 0.01 us  [body(): jnp.where(jnp.logical_and(~settled, lax.axis_index('seg') == 3), terminal...]
  transfers between devices with their start and end apart: 1 -> 11, of which waited for: 0 -> 8; matrix products, arithmetic and copies ran while one was open for 4% -> 0% of each run, Pallas kernels for 0% -> 5%
where the time goes in v1:
time: 42.5 us; the launch traced here: 41.8 us
  starting transfers between devices  16.5 us (39%)
  waiting for transfers between devices  15.7 us (37%)
  Pallas kernels  7.48 us (18%)
  between operations  1.38 us (3%)
  local copies, waits for them, and re-layouts  0.7 us (2%)
    ppermute x3, starting transfers between devices, apart(): return lax.ppermute(value, (axis, 'core'), pairs)  11.9 us
    ppermute x8, waiting for transfers between devices, swap(): lax.ppermute(value, axis, [(i, partner(i)) for i in range(lax.axis_size(a...  10.6 us
    pallas_call x9, Pallas kernels, call(): pl.pallas_call(kernel, out_shape=shapes, in_specs=[SMEM] * scalars + [VME...  7.48 us
    ppermute x3, waiting for transfers between devices, apart(): return lax.ppermute(value, (axis, 'core'), pairs)  5.06 us
    ppermute x8, starting transfers between devices, swap(): lax.ppermute(value, axis, [(i, partner(i)) for i in range(lax.axis_size(a...  4.67 us
  transfers between devices with their start and end apart: 11, of which 8 were waited for; matrix products, arithmetic and copies ran while one was open for 0% of the time, Pallas kernels for 5%

profile of v1, /device:TPU:2, one launch (start us, length us, event | category | flops | bytes accessed | tf_op | source)
XLA Modules:
  0.0 41.8 jit_solution(6342873051454244425)
XLA Ops:
  1.3 2.9 %shard_map.104 = (f32[136,128]{1,0:T(8,128)S(1)}, f32[4,136,128]{2,1,0:T(8,128)S(1)}) custom-call(s32[1]{0:T(128)S(6)} %copy.11.counts, f32[4,128,128]{2,1,0:T(8,128)} %jacobian.3, f32[4,128,128]{2,1,0:T(8,128)} %inverse.1, f32[4,64,128]{2,1,0:T(8,128)} %bitcast.4, f32[4,64]{1,0:T(4,128)} %controls.3, f32[4,64]{1,0:T(4,128)} %control_step.1, ...), custom_call_target="tpu_custom_call" | custom-call | bytes 400000 | tf_op jit(solution)/shard_map/pallas_call | solution.py:217
  4.2 0.1 collective-permute-start
  4.3 1.2 %collective-permute-done.other.refs_0_ = f32[136,128]{1,0:T(8,128)S(1)} collective-permute-done((f32[136,128]{1,0:T(8,128)S(1)}, f32[136,128]{1,0:T(8,128)S(1)}, u32[]{:S(2)}, u32[]{:S(2)}) %collective-permute-start) | collective-permute-done | bytes 69664 | tf_op jit(solution)/shard_map/ppermute | solution.py:201
  5.5 0.2 shard_map.105.own
  5.7 3.3 %collective-permute-start.1 = (f32[136,128]{1,0:T(8,128)S(1)}, f32[136,128]{1,0:T(8,128)S(1)}, u32[]{:S(2)}, u32[]{:S(2)}) collective-permute-start(f32[136,128]{1,0:T(8,128)S(1)} %shard_map.105.own), channel_id=1, source_target_pairs={{0,4},{1,3},{2,6},{3,1},{4,0},{5,7},{6,2},{7,5},{8,12},{9,11},{10,... | collective-permute-start | bytes 208904 | tf_op jit(solution)/shard_map/ppermute | solution.py:252
  9.0 1.1 %collective-permute-start.3 = (f32[136,128]{1,0:T(8,128)S(1)}, f32[136,128]{1,0:T(8,128)S(1)}, u32[]{:S(2)}, u32[]{:S(2)}) collective-permute-start(f32[136,128]{1,0:T(8,128)S(1)} %shard_map.105.own), channel_id=1, source_target_pairs={{0,6},{2,4},{4,2},{6,0},{1,7},{3,5},{5,3},{7,1},{8,14},{10,12},{12... | collective-permute-start | bytes 208904 | tf_op jit(solution)/shard_map/ppermute | solution.py:201
  10.0 2.2 %collective-permute-done.1.refs_1_.refs_2_ = f32[136,128]{1,0:T(8,128)S(1)} collective-permute-done((f32[136,128]{1,0:T(8,128)S(1)}, f32[136,128]{1,0:T(8,128)S(1)}, u32[]{:S(2)}, u32[]{:S(2)}) %collective-permute-start.1) | collective-permute-done | bytes 69664 | tf_op jit(solution)/shard_map/ppermute | solution.py:252
  12.2 0.0 collective-permute-start.2
  12.2 2.3 %collective-permute-done.3.refs_4_.refs_5_ = f32[136,128]{1,0:T(8,128)S(1)} collective-permute-done((f32[136,128]{1,0:T(8,128)S(1)}, f32[136,128]{1,0:T(8,128)S(1)}, u32[]{:S(2)}, u32[]{:S(2)}) %collective-permute-start.3) | collective-permute-done | bytes 69664 | tf_op jit(solution)/shard_map/ppermute | solution.py:201
  14.5 0.0 collective-permute-done.2.refs_0_.refs_3_
  14.5 0.4 shard_map.106
  14.9 2.0 %collective-permute-start.4 = (f32[136,128]{1,0:T(8,128)S(1)}, f32[136,128]{1,0:T(8,128)S(1)}, u32[]{:S(2)}, u32[]{:S(2)}) collective-permute-start(f32[136,128]{1,0:T(8,128)S(1)} %get-tuple-element.13.own), channel_id=1, source_target_pairs={{0,8},{8,0},{16,24},{24,16},{32,40},{40,32},{48,56},{56,48},{1,9},... | collective-permute-start | bytes 208904 | tf_op jit(solution)/shard_map/ppermute | solution.py:201
  16.9 2.4 %collective-permute-done.4.other.refs_3_ = f32[136,128]{1,0:T(8,128)S(1)} collective-permute-done((f32[136,128]{1,0:T(8,128)S(1)}, f32[136,128]{1,0:T(8,128)S(1)}, u32[]{:S(2)}, u32[]{:S(2)}) %collective-permute-start.4) | collective-permute-done | bytes 69664 | tf_op jit(solution)/shard_map/ppermute | solution.py:201
  19.3 0.2 shard_map.107.own
  19.5 0.0 copy-start
  19.5 6.4 %collective-permute-start.6 = (f32[136,128]{1,0:T(8,128)S(1)}, f32[136,128]{1,0:T(8,128)S(1)}, u32[]{:S(2)}, u32[]{:S(2)}) collective-permute-start(f32[136,128]{1,0:T(8,128)S(1)} %shard_map.107.own), channel_id=1, source_target_pairs={{0,48},{1,41},{8,56},{9,33},{16,32},{17,57},{24,40},{25,49},{32,16... | collective-permute-start | bytes 208904 | tf_op jit(solution)/shard_map/ppermute | solution.py:252
  25.9 1.5 %collective-permute-start.5 = (f32[136,128]{1,0:T(8,128)S(1)}, f32[136,128]{1,0:T(8,128)S(1)}, u32[]{:S(2)}, u32[]{:S(2)}) collective-permute-start(f32[136,128]{1,0:T(8,128)S(1)} %shard_map.107.own), channel_id=1, source_target_pairs={{0,16},{8,24},{16,0},{24,8},{32,48},{40,56},{48,32},{56,40},{1,17}... | collective-permute-start | bytes 208904 | tf_op jit(solution)/shard_map/ppermute | solution.py:201
  27.4 0.9 %collective-permute-done.6.refs_3_.refs_4_ = f32[136,128]{1,0:T(8,128)S(1)} collective-permute-done((f32[136,128]{1,0:T(8,128)S(1)}, f32[136,128]{1,0:T(8,128)S(1)}, u32[]{:S(2)}, u32[]{:S(2)}) %collective-permute-start.6) | collective-permute-done | bytes 69664 | tf_op jit(solution)/shard_map/ppermute | solution.py:252
  28.3 0.0 collective-permute-start.7
  28.3 3.6 %collective-permute-done.5.refs_0_.refs_1_ = f32[136,128]{1,0:T(8,128)S(1)} collective-permute-done((f32[136,128]{1,0:T(8,128)S(1)}, f32[136,128]{1,0:T(8,128)S(1)}, u32[]{:S(2)}, u32[]{:S(2)}) %collective-permute-start.5) | collective-permute-done | bytes 69664 | tf_op jit(solution)/shard_map/ppermute | solution.py:201
  31.9 0.0 collective-permute-done.7.refs_2_.refs_5_
  31.9 0.4 shard_map.108
  32.3 2.2 %collective-permute-start.8 = (f32[136,128]{1,0:T(8,128)S(1)}, f32[136,128]{1,0:T(8,128)S(1)}, u32[]{:S(2)}, u32[]{:S(2)}) collective-permute-start(f32[136,128]{1,0:T(8,128)S(1)} %get-tuple-element.14), channel_id=1, source_target_pairs={{0,128},{1,65},{64,192},{65,1},{128,0},{129,193},{192,64},{193,129... | collective-permute-start | bytes 208904 | tf_op jit(solution)/shard_map/ppermute | solution.py:252
  34.5 0.7 %copy-done.3 = f32[4,128]{1,0:T(4,128)S(1)} copy-done((f32[4,128]{1,0:T(4,128)S(1)}, f32[4,128]{1,0:T(4,128)}, u32[]{:S(2)}) %copy-start.3) | copy-done | bytes 2072
  35.2 0.0 copy-done.2
  35.2 1.0 %shard_map.111 = (f32[4,128]{1,0:T(4,128)S(1)}, f32[128,128]{1,0:T(8,128)S(1)}) custom-call(s32[1]{0:T(128)S(6)} %copy.11.counts, f32[4,128,128]{2,1,0:T(8,128)S(1)} %copy-done, f32[4,64,128]{2,1,0:T(8,128)S(1)} %bitcast.5, f32[4,64]{1,0:T(4,128)S(1)} %copy-done.2, f32[4,128]{1,0:T(4,128)S(1)} %copy-done.3), custom_call_target="tpu_custom_call" | custom-call | bytes 400000 | tf_op jit(solution)/shard_map/pallas_call | solution.py:217
  36.2 0.1 collective-permute-start.10
  36.3 2.0 %collective-permute-done.8.near_b.far_a = f32[136,128]{1,0:T(8,128)S(1)} collective-permute-done((f32[136,128]{1,0:T(8,128)S(1)}, f32[136,128]{1,0:T(8,128)S(1)}, u32[]{:S(2)}, u32[]{:S(2)}) %collective-permute-start.8) | collective-permute-done | bytes 69664 | tf_op jit(solution)/shard_map/ppermute | solution.py:252
  38.2 0.9 %shard_map.109.before = f32[136,128]{1,0:T(8,128)S(1)} custom-call(f32[136,128]{1,0:T(8,128)S(1)} %collective-permute-done.other.refs_0_, f32[136,128]{1,0:T(8,128)S(1)} %get-tuple-element.15.refs_1_, f32[136,128]{1,0:T(8,128)S(1)} %get-tuple-element.16.refs_2_, f32[136,128]{1,0:T(8,128)S(1)} %collective-permute-done.4.other.refs_3_, ...), custom_call_target="tpu_custom_call" | custom-call | bytes 400000 | tf_op jit(solution)/shard_map/pallas_call | solution.py:217
  39.1 0.3 shard_map.110.reach
  39.4 1.1 %collective-permute-done.10.cross = f32[136,128]{1,0:T(8,128)S(1)} collective-permute-done((f32[136,128]{1,0:T(8,128)S(1)}, f32[136,128]{1,0:T(8,128)S(1)}, u32[]{:S(2)}, u32[]{:S(2)}) %collective-permute-start.10) | collective-permute-done | bytes 69664 | tf_op jit(solution)/shard_map/ppermute | solution.py:201
  40.6 1.3 %shard_map.112 = (f32[4,128]{1,0:T(4,128)}, f32[4,128]{1,0:T(4,128)}) custom-call(s32[1]{0:T(128)S(6)} %copy.11.counts, f32[136,128]{1,0:T(8,128)S(1)} %collective-permute-done.9.near_a.far_b, f32[136,128]{1,0:T(8,128)S(1)} %collective-permute-done.8.near_b.far_a, f32[136,128]{1,0:T(8,128)S(1)} %collective-permute-done.8.near_b.far_a, ...), custom_call_target="tpu_custom_call" | custom-call | bytes 400000 | tf_op jit(solution)/shard_map/pallas_call | solution.py:217
  (10 shorter events, 0.0 us)
Async XLA Ops:
  4.2 1.3 %collective-permute-start = (f32[136,128]{1,0:T(8,128)S(1)}, f32[136,128]{1,0:T(8,128)S(1)}, u32[]{:S(2)}, u32[]{:S(2)}) collective-permute-start(f32[136,128]{1,0:T(8,128)S(1)} %get-tuple-element.12.own), channel_id=1, source_target_pairs={{0,1},{1,0},{2,3},{3,2},{4,5},{5,4},{6,7},{7,6},{8,9},{9,8},{10,11... | collective-permute-start | bytes 208904 | tf_op jit(solution)/shard_map/ppermute | solution.py:201
  5.7 6.5 %collective-permute-start.1 = (f32[136,128]{1,0:T(8,128)S(1)}, f32[136,128]{1,0:T(8,128)S(1)}, u32[]{:S(2)}, u32[]{:S(2)}) collective-permute-start(f32[136,128]{1,0:T(8,128)S(1)} %shard_map.105.own), channel_id=1, source_target_pairs={{0,4},{1,3},{2,6},{3,1},{4,0},{5,7},{6,2},{7,5},{8,12},{9,11},{10,... | collective-permute-start | bytes 208904 | tf_op jit(solution)/shard_map/ppermute | solution.py:252
  9.0 5.5 %collective-permute-start.3 = (f32[136,128]{1,0:T(8,128)S(1)}, f32[136,128]{1,0:T(8,128)S(1)}, u32[]{:S(2)}, u32[]{:S(2)}) collective-permute-start(f32[136,128]{1,0:T(8,128)S(1)} %shard_map.105.own), channel_id=1, source_target_pairs={{0,6},{2,4},{4,2},{6,0},{1,7},{3,5},{5,3},{7,1},{8,14},{10,12},{12... | collective-permute-start | bytes 208904 | tf_op jit(solution)/shard_map/ppermute | solution.py:201
  12.2 2.3 %collective-permute-start.2 = (f32[136,128]{1,0:T(8,128)S(1)}, f32[136,128]{1,0:T(8,128)S(1)}, u32[]{:S(2)}, u32[]{:S(2)}) collective-permute-start(f32[136,128]{1,0:T(8,128)S(1)} %collective-permute-done.1.refs_1_.refs_2_), channel_id=1, source_target_pairs={{0,1},{1,0},{2,3},{3,2},{4,5},{5,4},{6,7},{7,6},{8,9},{9,8},{10,11... | collective-permute-start | bytes 208904 | tf_op jit(solution)/shard_map/ppermute | solution.py:201
  14.9 4.4 %collective-permute-start.4 = (f32[136,128]{1,0:T(8,128)S(1)}, f32[136,128]{1,0:T(8,128)S(1)}, u32[]{:S(2)}, u32[]{:S(2)}) collective-permute-start(f32[136,128]{1,0:T(8,128)S(1)} %get-tuple-element.13.own), channel_id=1, source_target_pairs={{0,8},{8,0},{16,24},{24,16},{32,40},{40,32},{48,56},{56,48},{1,9},... | collective-permute-start | bytes 208904 | tf_op jit(solution)/shard_map/ppermute | solution.py:201
  19.5 15.0 %copy-start = (f32[4,128,128]{2,1,0:T(8,128)S(1)}, f32[4,128,128]{2,1,0:T(8,128)}, u32[]{:S(2)}) copy-start(f32[4,128,128]{2,1,0:T(8,128)} %jacobian.3) | copy-start | bytes 786436
  19.5 8.8 %collective-permute-start.6 = (f32[136,128]{1,0:T(8,128)S(1)}, f32[136,128]{1,0:T(8,128)S(1)}, u32[]{:S(2)}, u32[]{:S(2)}) collective-permute-start(f32[136,128]{1,0:T(8,128)S(1)} %shard_map.107.own), channel_id=1, source_target_pairs={{0,48},{1,41},{8,56},{9,33},{16,32},{17,57},{24,40},{25,49},{32,16... | collective-permute-start | bytes 208904 | tf_op jit(solution)/shard_map/ppermute | solution.py:252
  25.9 6.0 %collective-permute-start.5 = (f32[136,128]{1,0:T(8,128)S(1)}, f32[136,128]{1,0:T(8,128)S(1)}, u32[]{:S(2)}, u32[]{:S(2)}) collective-permute-start(f32[136,128]{1,0:T(8,128)S(1)} %shard_map.107.own), channel_id=1, source_target_pairs={{0,16},{8,24},{16,0},{24,8},{32,48},{40,56},{48,32},{56,40},{1,17}... | collective-permute-start | bytes 208904 | tf_op jit(solution)/shard_map/ppermute | solution.py:201
  28.3 3.6 %collective-permute-start.7 = (f32[136,128]{1,0:T(8,128)S(1)}, f32[136,128]{1,0:T(8,128)S(1)}, u32[]{:S(2)}, u32[]{:S(2)}) collective-permute-start(f32[136,128]{1,0:T(8,128)S(1)} %collective-permute-done.6.refs_3_.refs_4_), channel_id=1, source_target_pairs={{0,1},{1,0},{2,3},{3,2},{4,5},{5,4},{6,7},{7,6},{8,9},{9,8},{10,11... | collective-permute-start | bytes 208904 | tf_op jit(solution)/shard_map/ppermute | solution.py:201
  31.9 2.6 %copy-start.1 = (f32[4,128,64]{1,2,0:T(8,128)S(1)}, f32[4,128,64]{1,2,0:T(8,128)}, u32[]{:S(2)}) copy-start(f32[4,128,64]{1,2,0:T(8,128)} %param.11) | copy-start | bytes 393220
  32.3 5.9 %collective-permute-start.8 = (f32[136,128]{1,0:T(8,128)S(1)}, f32[136,128]{1,0:T(8,128)S(1)}, u32[]{:S(2)}, u32[]{:S(2)}) collective-permute-start(f32[136,128]{1,0:T(8,128)S(1)} %get-tuple-element.14), channel_id=1, source_target_pairs={{0,128},{1,65},{64,192},{65,1},{128,0},{129,193},{192,64},{193,129... | collective-permute-start | bytes 208904 | tf_op jit(solution)/shard_map/ppermute | solution.py:252
  34.5 0.7 %copy-start.3 = (f32[4,128]{1,0:T(4,128)S(1)}, f32[4,128]{1,0:T(4,128)}, u32[]{:S(2)}) copy-start(f32[4,128]{1,0:T(4,128)} %states.3) | copy-start | bytes 6148
  34.5 0.7 %copy-start.2 = (f32[4,64]{1,0:T(4,128)S(1)}, f32[4,64]{1,0:T(4,128)}, u32[]{:S(2)}) copy-start(f32[4,64]{1,0:T(4,128)} %controls.3) | copy-start | bytes 3076
  36.2 2.0 %copy-start.4 = (f32[128]{0:T(128)S(1)}, f32[128]{0:T(128)}, u32[]{:S(2)}) copy-start(f32[128]{0:T(128)} %param.15) | copy-start | bytes 1540
  36.2 4.4 %collective-permute-start.10 = (f32[136,128]{1,0:T(8,128)S(1)}, f32[136,128]{1,0:T(8,128)S(1)}, u32[]{:S(2)}, u32[]{:S(2)}) collective-permute-start(f32[136,128]{1,0:T(8,128)S(1)} %get-tuple-element.14), channel_id=1, source_target_pairs={{0,192},{64,128},{128,64},{192,0},{1,193},{65,129},{129,65},{193,1... | collective-permute-start | bytes 208904 | tf_op jit(solution)/shard_map/ppermute | solution.py:201
  38.2 2.3 %collective-permute-start.9 = (f32[136,128]{1,0:T(8,128)S(1)}, f32[136,128]{1,0:T(8,128)S(1)}, u32[]{:S(2)}, u32[]{:S(2)}) collective-permute-start(f32[136,128]{1,0:T(8,128)S(1)} %collective-permute-done.8.near_b.far_a), channel_id=1, source_target_pairs={{0,1},{1,0},{2,3},{3,2},{4,5},{5,4},{6,7},{7,6},{8,9},{9,8},{10,11... | collective-permute-start | bytes 208904 | tf_op jit(solution)/shard_map/ppermute | solution.py:201

commit v2 on v1

--- a/solution.py
+++ b/solution.py
@@ -55,8 +55,13 @@
     return jnp.where(row < width, out, jnp.where(row == width, out + later, earlier))
 
 
+def joined(earlier, later):
+    out = product(exact(earlier), exact(later[: earlier.shape[1]]))
+    return out + jnp.where(rows_of(out.shape) >= earlier.shape[1], later, 0.0)
+
+
 def maps_kernel(
-    counts, jacobian, inverse, input_map, controls, control_step, states, gap, total, partial
+    counts, jacobian, inverse, input_map, controls, control_step, states, gap, total, *slots
 ):
     knots, width = states.shape
     first = jnp.bool_(True)
@@ -66,25 +71,26 @@
     row = rows_of((ROWS, width))
     eye = eye_of((ROWS, width))
     drive = exact(controls[...] + control_step[...])
-    running = None
+    steps = []
     for k in range(knots):
-        pushed = product(drive, exact(input_map[k]))
+        pushed = product(drive, exact(input_map[k]))[k : k + 1]
+        fixed = eye
+        if k == 0:
+            pushed += product(exact(jnp.broadcast_to(start, (8, width))), exact(jacobian[k]), NT)[0:1]
+            fixed = eye + jnp.where(row >= width, jnp.broadcast_to(start, eye.shape), 0.0)
         left = jnp.concatenate(
-            [jacobian[k].T, jnp.broadcast_to(pushed[k : k + 1], (ROWS - width, width))], axis=0
+            [jacobian[k].T, jnp.broadcast_to(pushed, (ROWS - width, width))], axis=0
         )
-        step = product(exact(left), exact(inverse[k]), NT) + eye
-        step = jnp.where(k < counts[0], step, eye)
-        matrix = exact(step[:width])
-        if k == 0:
-            moved = product(exact(jnp.broadcast_to(start, (8, width))), matrix)
-            running = step + jnp.where(row >= width, jnp.broadcast_to(moved[0:1], step.shape), 0.0)
-        else:
-            running = product(exact(running), matrix) + jnp.where(row >= width, step, 0.0)
-        partial[k] = running
-    total[...] = jnp.where(row == width + 1, jnp.broadcast_to(states[0:1, :], running.shape), running)
-
-
-def defect_kernel(counts, jacobian, input_map, controls, states, base, last):
+        step = product(exact(left), exact(inverse[k]), NT) + fixed
+        steps.append(step if k < knots // 2 else jnp.where(k < counts[0], step, eye))
+    half = joined(steps[0], steps[1])
+    whole = joined(half, joined(steps[2], steps[3]))
+    for ref, value in zip(slots, (steps[0], half, steps[2], whole)):
+        ref[...] = value
+    total[...] = jnp.where(row == width + 1, jnp.broadcast_to(states[0:1, :], whole.shape), whole)
+
+
+def defect_kernel(counts, jacobian, input_map, controls, states, half, step, base, last, third):
     knots, width = states.shape
     count = counts[0]
     slot = rows_of((knots, width))
@@ -109,6 +115,7 @@
         )
     base[...] = jnp.where(slot < count, jnp.concatenate(rows, axis=0), 0.0)
     last[...] = jacobian[count - 1]
+    third[...] = joined(half[...], step[...])
 
 
 def pair_kernel(axis, own, other, total):
@@ -117,19 +124,22 @@
     total[...] = compose(jnp.where(odd, theirs, mine), jnp.where(odd, mine, theirs))
 
 
-def choose(pair):
-    if pair[0] is pair[1]:
-        return pair[0][...]
-    return jnp.where(lax.axis_index("core") == 0, pair[0][...], pair[1][...])
-
-
-def four_kernel(axis, shift, own, *refs):
-    near, far, cross = refs[0:2], refs[2:4], refs[4:6]
-    total, beside, others = refs[6:]
+def arrived(own, passed, common):
+    first = lax.axis_index("core") == 0
+    return jnp.where(first, own, passed), jnp.where(first, passed, own), common
+
+
+def four_kernel(axis, shift, ring, own, *refs):
+    total, beside, others = refs[-3:]
     place = lax.axis_index(axis) >> shift
     odd = place % 2 == 1
     high = place >= 2
-    a, b, c, d = own[...], choose(near), choose(far), choose(cross)
+    a = own[...]
+    behind, c, ahead = arrived(*(ref[...] for ref in refs[:3]))
+    if ring:
+        b, d = jnp.where(odd, behind, ahead), jnp.where(odd, ahead, behind)
+    else:
+        b, d = ahead, behind
     beside[...] = b
     mine = compose(jnp.where(odd, b, a), jnp.where(odd, a, b))
     rest = compose(jnp.where(odd, d, c), jnp.where(odd, c, d))
@@ -148,36 +158,33 @@
     out[...] = before
 
 
-def reach_kernel(before, partial, reach):
+def reach_kernel(before, *refs):
+    reach = refs[-1]
     width = before.shape[1]
     row = rows_of(before.shape)
     left = parts(before[...])
-    for k in range(partial.shape[0]):
-        reach[k] = product(left, parts(partial[k, :width])) + jnp.where(row == width, partial[k], 0.0)
-
-
-def final_kernel(
-    counts, near_a, near_b, far_a, far_b, cross, reach, upcoming, base, last, updated, defect
-):
+    for k, ref in enumerate(refs[:-1]):
+        reach[k] = product(left, parts(ref[:width])) + jnp.where(row == width, ref[...], 0.0)
+
+
+def final_kernel(counts, reach, upcoming, base, last, own, passed, common, updated, defect):
     knots, width = base.shape
-    near, far = choose((near_a, near_b)), choose((far_a, far_b))
     x = lax.axis_index("seg")
     count = counts[0]
     slot = rows_of((knots, width))
-    start = jnp.where(
-        x == 3,
-        cross[width : width + 1],
-        jnp.where(x == 2, far[width : width + 1], jnp.where(x == 1, near[width : width + 1], 0.0)),
-    )
+    back, back2, ahead = arrived(own[...], passed[...], common[...])
 
     def wide(row):
         return jnp.broadcast_to(row, (8, width))
 
-    second = jnp.where(x == 3, far, cross[...])
-    moved = product(parts(wide(start)), parts(second[:width]))[0:1] + second[width : width + 1]
-    start = jnp.where(x >= 2, moved, start)
-    moved = product(parts(wide(start)), parts(near[:width]))[0:1] + near[width : width + 1]
-    start = parts(wide(jnp.where(x == 3, moved, start)))
+    def moved(start, way):
+        return product(parts(wide(start)), parts(way[:width]))[0:1] + way[width : width + 1]
+
+    start = jnp.where(x == 3, ahead, jnp.where(x == 2, back2, back))[width : width + 1]
+    start = jnp.where(x == 0, 0.0, start)
+    start = jnp.where(x >= 2, moved(start, jnp.where(x == 3, back2, back)), start)
+    start = jnp.where(x == 3, moved(start, back), start)
+    start = parts(wide(start))
     for k in range(knots):
         state = product(start, parts(reach[k, :width]))[0:1] + reach[k, width : width + 1]
         updated[k : k + 1] = jnp.where(k < count, state, 0.0)
@@ -187,8 +194,7 @@
             jnp.logical_and(lax.axis_index("y") == 3, lax.axis_index("core") == 1),
         )
     )
-    lead = width + 1
-    after = jnp.where(x == 1, cross[lead : lead + 1], near[lead : lead + 1])
+    after = ahead[width + 1 : width + 2]
     after = jnp.where(jnp.logical_or(settled, x == 3), upcoming[...], after)
     matrix = parts(last[...])
     once = product(parts(wide(after)), matrix, NT)
@@ -229,18 +235,18 @@
     z, _, core = (lax.axis_index(name) for name in AXES[1:])
     square = (ROWS, width)
     input_map = jnp.swapaxes(input_map, 1, 2)
-    total, partial = call(
+    total, step, half, third, whole = call(
         maps_kernel,
-        [square, (knots, *square)],
+        [square] * 5,
         (counts, jacobian, inverse, input_map, controls, control_step, states, gap[None]),
         scalars=1,
     )
-    base, last = call(
+    base, last, third = call(
         defect_kernel,
-        [(knots, width), (width, width)],
-        (counts, jacobian, input_map, controls, states),
+        [(knots, width), (width, width), square],
+        (counts, jacobian, input_map, controls, states, half, third),
         scalars=1,
-        held=range(1, 5),
+        held=range(1, 7),
     )
 
     def lead(pieces):
@@ -261,59 +267,56 @@
     settled = core == 0
     total = call(functools.partial(pair_kernel, "core"), square, (total, other), held=(0, 1))
 
-    def gathered(total, axis, masks, shared, first):
+    def gathered(total, axis, partners, shared, late):
         def both():
-            return swap(total, axis, lambda i: i ^ shared)
-
-        def each():
-            return apart(total, axis, [lambda i, d=d: i ^ d for d in masks])
-
-        if first:
-            common, own = both(), each()
-        else:
-            own, common = each(), both()
+            return swap(total, axis, shared)
+
+        common = None if late else both()
+        own = apart(total, axis, partners)
+        common = both() if late else common
         passed = across(own)
-        return {shared: (common, common), masks[0]: (own, passed), masks[1]: (passed, own)}
-
-    def one(arrival):
-        return jnp.where(core == 0, lead(arrival[0]), lead(arrival[1]))
-
-    def four(total, upcoming, settled, axis, shift, arrivals):
+        return own, passed, common
+
+    def four(total, upcoming, settled, axis, shift, ring, found):
         place = lax.axis_index(axis) >> shift
-        operands = [total]
-        for arrival in arrivals:
-            operands.extend(arrival)
         whole, near, others = call(
-            functools.partial(four_kernel, axis, shift), [square, square, square], operands, held=range(7)
+            functools.partial(four_kernel, axis, shift, ring),
+            [square, square, square],
+            [total, *found],
+            held=range(4),
         )
-        after = jnp.where(place % 2 == 1, one(arrivals[2]), one(arrivals[0]))
+        behind, _, ahead = arrived(*map(lead, found))
+        after = ahead if ring else jnp.where(place % 2 == 1, behind, ahead)
         upcoming = jnp.where(settled, upcoming, after)
         settled = jnp.logical_or(settled, place < 3)
         levels.extend([(axis, shift), (axis, shift + 1)])
         earlier.extend([near, others])
         return whole, upcoming, settled
 
-    found = gathered(total, "y", (2, 1), 3, False)
-    total, upcoming, settled = four(total, upcoming, settled, "y", 0, [found[1], found[2], found[3]])
+    ring = ([lambda i: (i + 1) % 4, lambda i: (i + 2) % 4], lambda i: (i + 3) % 4)
+    found = gathered(total, "y", *ring, True)
+    total, upcoming, settled = four(total, upcoming, settled, "y", 0, True, found)
     levels.append(("z", 0))
     other = swap(total, "z", lambda i: i ^ 1)
     earlier.append(other)
     upcoming = jnp.where(settled, upcoming, lead(other))
     settled = jnp.logical_or(settled, z % 2 == 0)
     total = call(functools.partial(pair_kernel, "z"), square, (total, other), held=(0, 1))
-    found = gathered(total, "z", (6, 5), 2, True)
-    total, upcoming, settled = four(total, upcoming, settled, "z", 1, [found[2], found[5], found[6]])
+    found = gathered(total, "z", [lambda i: i ^ 6, lambda i: i ^ 5], lambda i: i ^ 2, False)
+    total, upcoming, settled = four(total, upcoming, settled, "z", 1, False, found)
     upcoming = jnp.where(jnp.logical_and(~settled, lax.axis_index("seg") == 3), terminal[None], upcoming)
-    found = gathered(total, "seg", (2, 1), 3, False)
-    before = call(functools.partial(before_kernel, levels), square, earlier, held=range(len(earlier)))
-    reach = call(reach_kernel, (knots, *square), (before, partial), held=(0, 1))
+    found = gathered(total, "seg", [ring[0][0], lambda i: (2, 3, 1, 0)[i]], ring[1], True)
+    before = call(
+        functools.partial(before_kernel, levels), square, earlier, held=range(len(earlier))
+    )
+    reach = call(reach_kernel, (knots, *square), (before, step, half, third, whole), held=range(5))
     updated, defect = call(
         final_kernel,
         [(knots, width), (knots, width)],
-        (counts, *found[1], *found[2], *found[3][:1], reach, upcoming, base, last),
+        (counts, reach, upcoming, base, last, *found),
         scalars=1,
         local=False,
-        held=range(1, 10),
+        held=range(1, 8),
     )
     return updated, defect
 

time: 42.5 us -> 39.8 us (0.936)
  starting transfers between devices: 16.5 us -> 15.3 us
  waiting for transfers between devices: 15.7 us -> 14.6 us
  Pallas kernels: 7.48 us -> 7.02 us
    ppermute x3, starting transfers between devices: 11.9 us -> 9.5 us  [apart(): return lax.ppermute(value, (axis, 'core'), pairs)]
    ppermute x8, starting transfers between devices: 4.67 us -> 5.83 us  [swap(): lax.ppermute(value, axis, [(i, partner(i)) for i in range(lax.axis_size(a...]
    ppermute x8, waiting for transfers between devices: 10.6 us -> 10.1 us  [swap(): lax.ppermute(value, axis, [(i, partner(i)) for i in range(lax.axis_size(a...]
    ppermute x3, waiting for transfers between devices: 5.06 us -> 4.52 us  [apart(): return lax.ppermute(value, (axis, 'core'), pairs)]
    pallas_call x9, Pallas kernels: 7.48 us -> 7.02 us  [call(): pl.pallas_call(kernel, out_shape=shapes, in_specs=[SMEM] * scalars + [VME...]
  transfers between devices with their start and end apart: 11 -> 11, of which waited for: 8 -> 9; matrix products, arithmetic and copies ran while one was open for 0% -> 0% of each run, Pallas kernels for 5% -> 6%
where the time goes in v2:
time: 39.8 us; the launch traced here: 39 us
  starting transfers between devices  15.3 us (38%)
  waiting for transfers between devices  14.6 us (37%)
  Pallas kernels  7.02 us (18%)
  between operations  1.39 us (3%)
  local copies, waits for them, and re-layouts  0.7 us (2%)
    ppermute x8, waiting for transfers between devices, swap(): lax.ppermute(value, axis, [(i, partner(i)) for i in range(lax.axis_size(a...  10.1 us
    ppermute x3, starting transfers between devices, apart(): return lax.ppermute(value, (axis, 'core'), pairs)  9.5 us
    pallas_call x9, Pallas kernels, call(): pl.pallas_call(kernel, out_shape=shapes, in_specs=[SMEM] * scalars + [VME...  7.02 us
    ppermute x8, starting transfers between devices, swap(): lax.ppermute(value, axis, [(i, partner(i)) for i in range(lax.axis_size(a...  5.83 us
    ppermute x3, waiting for transfers between devices, apart(): return lax.ppermute(value, (axis, 'core'), pairs)  4.52 us
  transfers between devices with their start and end apart: 11, of which 9 were waited for; matrix products, arithmetic and copies ran while one was open for 0% of the time, Pallas kernels for 6%

profile of v2, /device:TPU:2, one launch (start us, length us, event | category | flops | bytes accessed | tf_op | source)
XLA Modules:
  0.0 39.0 jit_solution(3826513986690706696)
XLA Ops:
  1.3 2.4 %shard_map.104 = (f32[136,128]{1,0:T(8,128)S(1)}, f32[136,128]{1,0:T(8,128)S(1)}, f32[136,128]{1,0:T(8,128)S(1)}, f32[136,128]{1,0:T(8,128)S(1)}, f32[136,128]{1,0:T(8,128)S(1)}) custom-call(s32[1]{0:T(128)S(6)} %copy.11.counts, f32[4,128,128]{2,1,0:T(8,128)} %jacobian.3, f32[4,128,128]{2,1,0:T(8,128)} %inverse.1, f32[4,64,128]{2,1,0:T(8,128)} %bitcast.4, ...), custom_call_target="tpu_custom_call" | custom-call | bytes 400000 | tf_op jit(solution)/shard_map/pallas_call | solution.py:223
  3.6 0.1 collective-permute-start
  3.7 1.2 %collective-permute-done.other.refs_0_ = f32[136,128]{1,0:T(8,128)S(1)} collective-permute-done((f32[136,128]{1,0:T(8,128)S(1)}, f32[136,128]{1,0:T(8,128)S(1)}, u32[]{:S(2)}, u32[]{:S(2)}) %collective-permute-start) | collective-permute-done | bytes 69664 | tf_op jit(solution)/shard_map/ppermute | solution.py:207
  5.0 0.2 shard_map.105.own
  5.2 1.7 %collective-permute-start.1 = (f32[136,128]{1,0:T(8,128)S(1)}, f32[136,128]{1,0:T(8,128)S(1)}, u32[]{:S(2)}, u32[]{:S(2)}) collective-permute-start(f32[136,128]{1,0:T(8,128)S(1)} %shard_map.105.own), channel_id=1, source_target_pairs={{0,2},{1,5},{2,4},{3,7},{4,6},{5,1},{6,0},{7,3},{8,10},{9,13},{10,... | collective-permute-start | bytes 208904 | tf_op jit(solution)/shard_map/ppermute | solution.py:258
  6.8 1.7 %collective-permute-start.3 = (f32[136,128]{1,0:T(8,128)S(1)}, f32[136,128]{1,0:T(8,128)S(1)}, u32[]{:S(2)}, u32[]{:S(2)}) collective-permute-start(f32[136,128]{1,0:T(8,128)S(1)} %shard_map.105.own), channel_id=1, source_target_pairs={{0,6},{2,0},{4,2},{6,4},{1,7},{3,1},{5,3},{7,5},{8,14},{10,8},{12,... | collective-permute-start | bytes 208904 | tf_op jit(solution)/shard_map/ppermute | solution.py:207
  8.5 2.5 %collective-permute-done.1.refs_0_ = f32[136,128]{1,0:T(8,128)S(1)} collective-permute-done((f32[136,128]{1,0:T(8,128)S(1)}, f32[136,128]{1,0:T(8,128)S(1)}, u32[]{:S(2)}, u32[]{:S(2)}) %collective-permute-start.1) | collective-permute-done | bytes 69664 | tf_op jit(solution)/shard_map/ppermute | solution.py:258
  11.0 0.8 %collective-permute-done.3.refs_2_ = f32[136,128]{1,0:T(8,128)S(1)} collective-permute-done((f32[136,128]{1,0:T(8,128)S(1)}, f32[136,128]{1,0:T(8,128)S(1)}, u32[]{:S(2)}, u32[]{:S(2)}) %collective-permute-start.3) | collective-permute-done | bytes 69664 | tf_op jit(solution)/shard_map/ppermute | solution.py:207
  11.8 0.5 %collective-permute-done.2.refs_1_ = f32[136,128]{1,0:T(8,128)S(1)} collective-permute-done((f32[136,128]{1,0:T(8,128)S(1)}, f32[136,128]{1,0:T(8,128)S(1)}, u32[]{:S(2)}, u32[]{:S(2)}) %collective-permute-start.2) | collective-permute-done | bytes 69664 | tf_op jit(solution)/shard_map/ppermute | solution.py:207
  12.3 0.4 %shard_map.106 = (f32[136,128]{1,0:T(8,128)S(1)}, f32[136,128]{1,0:T(8,128)S(1)}, f32[136,128]{1,0:T(8,128)S(1)}) custom-call(f32[136,128]{1,0:T(8,128)S(1)} %shard_map.105.own, f32[136,128]{1,0:T(8,128)S(1)} %collective-permute-done.1.refs_0_, f32[136,128]{1,0:T(8,128)S(1)} %collective-permute-done.2.refs_1_, f32[136,128]{1,0:T(8,128)S(1)} %collective-permute-done.3.refs_2_), custom_call_target="tpu_custom_call" | custom-call | bytes 400000 | tf_op jit(solution)/shard_map/pallas_call | solution.py:223
  12.7 0.0 copy-start
  12.7 2.0 %collective-permute-start.4 = (f32[136,128]{1,0:T(8,128)S(1)}, f32[136,128]{1,0:T(8,128)S(1)}, u32[]{:S(2)}, u32[]{:S(2)}) collective-permute-start(f32[136,128]{1,0:T(8,128)S(1)} %get-tuple-element.19.own), channel_id=1, source_target_pairs={{0,8},{8,0},{16,24},{24,16},{32,40},{40,32},{48,56},{56,48},{1,9},... | collective-permute-start | bytes 208904 | tf_op jit(solution)/shard_map/ppermute | solution.py:207
  14.7 2.5 %collective-permute-done.4.other.refs_3_ = f32[136,128]{1,0:T(8,128)S(1)} collective-permute-done((f32[136,128]{1,0:T(8,128)S(1)}, f32[136,128]{1,0:T(8,128)S(1)}, u32[]{:S(2)}, u32[]{:S(2)}) %collective-permute-start.4) | collective-permute-done | bytes 69664 | tf_op jit(solution)/shard_map/ppermute | solution.py:207
  17.2 0.2 shard_map.107.own
  17.4 0.0 copy-start.1
  17.4 6.3 %collective-permute-start.5 = (f32[136,128]{1,0:T(8,128)S(1)}, f32[136,128]{1,0:T(8,128)S(1)}, u32[]{:S(2)}, u32[]{:S(2)}) collective-permute-start(f32[136,128]{1,0:T(8,128)S(1)} %shard_map.107.own), channel_id=1, source_target_pairs={{0,48},{1,41},{8,56},{9,33},{16,32},{17,57},{24,40},{25,49},{32,16... | collective-permute-start | bytes 208904 | tf_op jit(solution)/shard_map/ppermute | solution.py:258
  23.7 1.5 %collective-permute-start.7 = (f32[136,128]{1,0:T(8,128)S(1)}, f32[136,128]{1,0:T(8,128)S(1)}, u32[]{:S(2)}, u32[]{:S(2)}) collective-permute-start(f32[136,128]{1,0:T(8,128)S(1)} %shard_map.107.own), channel_id=1, source_target_pairs={{0,16},{8,24},{16,0},{24,8},{32,48},{40,56},{48,32},{56,40},{1,17}... | collective-permute-start | bytes 208904 | tf_op jit(solution)/shard_map/ppermute | solution.py:207
  25.2 1.6 %collective-permute-done.5.refs_0_ = f32[136,128]{1,0:T(8,128)S(1)} collective-permute-done((f32[136,128]{1,0:T(8,128)S(1)}, f32[136,128]{1,0:T(8,128)S(1)}, u32[]{:S(2)}, u32[]{:S(2)}) %collective-permute-start.5) | collective-permute-done | bytes 69664 | tf_op jit(solution)/shard_map/ppermute | solution.py:258
  26.7 2.9 %collective-permute-done.7.refs_2_ = f32[136,128]{1,0:T(8,128)S(1)} collective-permute-done((f32[136,128]{1,0:T(8,128)S(1)}, f32[136,128]{1,0:T(8,128)S(1)}, u32[]{:S(2)}, u32[]{:S(2)}) %collective-permute-start.7) | collective-permute-done | bytes 69664 | tf_op jit(solution)/shard_map/ppermute | solution.py:207
  29.6 0.0 collective-permute-done.6.refs_1_
  29.6 0.4 %shard_map.108 = (f32[136,128]{1,0:T(8,128)S(1)}, f32[136,128]{1,0:T(8,128)S(1)}, f32[136,128]{1,0:T(8,128)S(1)}) custom-call(f32[136,128]{1,0:T(8,128)S(1)} %shard_map.107.own, f32[136,128]{1,0:T(8,128)S(1)} %collective-permute-done.5.refs_0_, f32[136,128]{1,0:T(8,128)S(1)} %collective-permute-done.6.refs_1_, f32[136,128]{1,0:T(8,128)S(1)} %collective-permute-done.7.refs_2_), custom_call_target="tpu_custom_call" | custom-call | bytes 400000 | tf_op jit(solution)/shard_map/pallas_call | solution.py:223
  30.1 1.6 %collective-permute-start.8 = (f32[136,128]{1,0:T(8,128)S(1)}, f32[136,128]{1,0:T(8,128)S(1)}, u32[]{:S(2)}, u32[]{:S(2)}) collective-permute-start(f32[136,128]{1,0:T(8,128)S(1)} %get-tuple-element.29), channel_id=1, source_target_pairs={{0,64},{1,129},{64,128},{65,193},{128,192},{129,65},{192,0},{193,1... | collective-permute-start | bytes 208904 | tf_op jit(solution)/shard_map/ppermute | solution.py:258
  31.6 0.7 %copy-done.3 = f32[4,128]{1,0:T(4,128)S(1)} copy-done((f32[4,128]{1,0:T(4,128)S(1)}, f32[4,128]{1,0:T(4,128)}, u32[]{:S(2)}) %copy-start.3) | copy-done | bytes 2072
  32.3 0.0 copy-done.2
  32.3 1.1 %shard_map.110 = (f32[4,128]{1,0:T(4,128)S(1)}, f32[128,128]{1,0:T(8,128)S(1)}, f32[136,128]{1,0:T(8,128)S(1)}) custom-call(s32[1]{0:T(128)S(6)} %copy.11.counts, f32[4,128,128]{2,1,0:T(8,128)S(1)} %copy-done, f32[4,64,128]{2,1,0:T(8,128)S(1)} %bitcast.5, f32[4,64]{1,0:T(4,128)S(1)} %copy-done.2, f32[4,128]{1,0:T(4,128)S(1)} %copy-done.3, ...), custom_call_target="tpu_custom_call" | custom-call | bytes 400000 | tf_op jit(solution)/shard_map/pallas_call | solution.py:223
  33.4 0.6 %collective-permute-start.10 = (f32[136,128]{1,0:T(8,128)S(1)}, f32[136,128]{1,0:T(8,128)S(1)}, u32[]{:S(2)}, u32[]{:S(2)}) collective-permute-start(f32[136,128]{1,0:T(8,128)S(1)} %get-tuple-element.29), channel_id=1, source_target_pairs={{0,192},{64,0},{128,64},{192,128},{1,193},{65,1},{129,65},{193,129... | collective-permute-start | bytes 208904 | tf_op jit(solution)/shard_map/ppermute | solution.py:207
  34.0 0.4 %collective-permute-done.8.own = f32[136,128]{1,0:T(8,128)S(1)} collective-permute-done((f32[136,128]{1,0:T(8,128)S(1)}, f32[136,128]{1,0:T(8,128)S(1)}, u32[]{:S(2)}, u32[]{:S(2)}) %collective-permute-start.8) | collective-permute-done | bytes 69664 | tf_op jit(solution)/shard_map/ppermute | solution.py:258
  34.4 0.0 collective-permute-start.9
  34.5 0.9 %shard_map.109.before = f32[136,128]{1,0:T(8,128)S(1)} custom-call(f32[136,128]{1,0:T(8,128)S(1)} %collective-permute-done.other.refs_0_, f32[136,128]{1,0:T(8,128)S(1)} %get-tuple-element.17.refs_1_, f32[136,128]{1,0:T(8,128)S(1)} %get-tuple-element.18.refs_2_, f32[136,128]{1,0:T(8,128)S(1)} %collective-permute-done.4.other.refs_3_, ...), custom_call_target="tpu_custom_call" | custom-call | bytes 400000 | tf_op jit(solution)/shard_map/pallas_call | solution.py:223
  35.3 0.3 shard_map.111.reach
  35.7 2.1 %collective-permute-done.10.common = f32[136,128]{1,0:T(8,128)S(1)} collective-permute-done((f32[136,128]{1,0:T(8,128)S(1)}, f32[136,128]{1,0:T(8,128)S(1)}, u32[]{:S(2)}, u32[]{:S(2)}) %collective-permute-start.10) | collective-permute-done | bytes 69664 | tf_op jit(solution)/shard_map/ppermute | solution.py:207
  37.8 1.2 %shard_map.112 = (f32[4,128]{1,0:T(4,128)}, f32[4,128]{1,0:T(4,128)}) custom-call(s32[1]{0:T(128)S(6)} %copy.11.counts, f32[4,136,128]{2,1,0:T(8,128)S(1)} %shard_map.111.reach, f32[1,128]{1,0:T(1,128)S(1)} %broadcast_select_fusion.5.upcoming, f32[4,128]{1,0:T(4,128)S(1)} %get-tuple-element.27.base, f32[128,128]{1,0:T(8,128)S(1)} %get-tuple-element.28.last, ...), custom_call_target="tpu_custom_call" | custom-call | bytes 400000 | tf_op jit(solution)/shard_map/pallas_call | solution.py:223
  (10 shorter events, 0.0 us)
Async XLA Ops:
  3.6 1.3 %collective-permute-start = (f32[136,128]{1,0:T(8,128)S(1)}, f32[136,128]{1,0:T(8,128)S(1)}, u32[]{:S(2)}, u32[]{:S(2)}) collective-permute-start(f32[136,128]{1,0:T(8,128)S(1)} %get-tuple-element.16.own), channel_id=1, source_target_pairs={{0,1},{1,0},{2,3},{3,2},{4,5},{5,4},{6,7},{7,6},{8,9},{9,8},{10,11... | collective-permute-start | bytes 208904 | tf_op jit(solution)/shard_map/ppermute | solution.py:207
  5.2 5.8 %collective-permute-start.1 = (f32[136,128]{1,0:T(8,128)S(1)}, f32[136,128]{1,0:T(8,128)S(1)}, u32[]{:S(2)}, u32[]{:S(2)}) collective-permute-start(f32[136,128]{1,0:T(8,128)S(1)} %shard_map.105.own), channel_id=1, source_target_pairs={{0,2},{1,5},{2,4},{3,7},{4,6},{5,1},{6,0},{7,3},{8,10},{9,13},{10,... | collective-permute-start | bytes 208904 | tf_op jit(solution)/shard_map/ppermute | solution.py:258
  6.8 4.9 %collective-permute-start.3 = (f32[136,128]{1,0:T(8,128)S(1)}, f32[136,128]{1,0:T(8,128)S(1)}, u32[]{:S(2)}, u32[]{:S(2)}) collective-permute-start(f32[136,128]{1,0:T(8,128)S(1)} %shard_map.105.own), channel_id=1, source_target_pairs={{0,6},{2,0},{4,2},{6,4},{1,7},{3,1},{5,3},{7,5},{8,14},{10,8},{12,... | collective-permute-start | bytes 208904 | tf_op jit(solution)/shard_map/ppermute | solution.py:207
  11.0 1.3 %collective-permute-start.2 = (f32[136,128]{1,0:T(8,128)S(1)}, f32[136,128]{1,0:T(8,128)S(1)}, u32[]{:S(2)}, u32[]{:S(2)}) collective-permute-start(f32[136,128]{1,0:T(8,128)S(1)} %collective-permute-done.1.refs_0_), channel_id=1, source_target_pairs={{0,1},{1,0},{2,3},{3,2},{4,5},{5,4},{6,7},{7,6},{8,9},{9,8},{10,11... | collective-permute-start | bytes 208904 | tf_op jit(solution)/shard_map/ppermute | solution.py:207
  12.7 19.0 %copy-start = (f32[4,128,128]{2,1,0:T(8,128)S(1)}, f32[4,128,128]{2,1,0:T(8,128)}, u32[]{:S(2)}) copy-start(f32[4,128,128]{2,1,0:T(8,128)} %jacobian.3) | copy-start | bytes 786436
  12.7 4.5 %collective-permute-start.4 = (f32[136,128]{1,0:T(8,128)S(1)}, f32[136,128]{1,0:T(8,128)S(1)}, u32[]{:S(2)}, u32[]{:S(2)}) collective-permute-start(f32[136,128]{1,0:T(8,128)S(1)} %get-tuple-element.19.own), channel_id=1, source_target_pairs={{0,8},{8,0},{16,24},{24,16},{32,40},{40,32},{48,56},{56,48},{1,9},... | collective-permute-start | bytes 208904 | tf_op jit(solution)/shard_map/ppermute | solution.py:207
  17.4 14.2 %copy-start.1 = (f32[4,128,64]{1,2,0:T(8,128)S(1)}, f32[4,128,64]{1,2,0:T(8,128)}, u32[]{:S(2)}) copy-start(f32[4,128,64]{1,2,0:T(8,128)} %param.11) | copy-start | bytes 393220
  17.4 9.3 %collective-permute-start.5 = (f32[136,128]{1,0:T(8,128)S(1)}, f32[136,128]{1,0:T(8,128)S(1)}, u32[]{:S(2)}, u32[]{:S(2)}) collective-permute-start(f32[136,128]{1,0:T(8,128)S(1)} %shard_map.107.own), channel_id=1, source_target_pairs={{0,48},{1,41},{8,56},{9,33},{16,32},{17,57},{24,40},{25,49},{32,16... | collective-permute-start | bytes 208904 | tf_op jit(solution)/shard_map/ppermute | solution.py:258
  23.7 6.0 %collective-permute-start.7 = (f32[136,128]{1,0:T(8,128)S(1)}, f32[136,128]{1,0:T(8,128)S(1)}, u32[]{:S(2)}, u32[]{:S(2)}) collective-permute-start(f32[136,128]{1,0:T(8,128)S(1)} %shard_map.107.own), channel_id=1, source_target_pairs={{0,16},{8,24},{16,0},{24,8},{32,48},{40,56},{48,32},{56,40},{1,17}... | collective-permute-start | bytes 208904 | tf_op jit(solution)/shard_map/ppermute | solution.py:207
  26.7 2.9 %collective-permute-start.6 = (f32[136,128]{1,0:T(8,128)S(1)}, f32[136,128]{1,0:T(8,128)S(1)}, u32[]{:S(2)}, u32[]{:S(2)}) collective-permute-start(f32[136,128]{1,0:T(8,128)S(1)} %collective-permute-done.5.refs_0_), channel_id=1, source_target_pairs={{0,1},{1,0},{2,3},{3,2},{4,5},{5,4},{6,7},{7,6},{8,9},{9,8},{10,11... | collective-permute-start | bytes 208904 | tf_op jit(solution)/shard_map/ppermute | solution.py:207
  30.1 4.4 %collective-permute-start.8 = (f32[136,128]{1,0:T(8,128)S(1)}, f32[136,128]{1,0:T(8,128)S(1)}, u32[]{:S(2)}, u32[]{:S(2)}) collective-permute-start(f32[136,128]{1,0:T(8,128)S(1)} %get-tuple-element.29), channel_id=1, source_target_pairs={{0,64},{1,129},{64,128},{65,193},{128,192},{129,65},{192,0},{193,1... | collective-permute-start | bytes 208904 | tf_op jit(solution)/shard_map/ppermute | solution.py:258
  31.6 0.7 %copy-start.3 = (f32[4,128]{1,0:T(4,128)S(1)}, f32[4,128]{1,0:T(4,128)}, u32[]{:S(2)}) copy-start(f32[4,128]{1,0:T(4,128)} %states.3) | copy-start | bytes 6148
  31.6 0.7 %copy-start.2 = (f32[4,64]{1,0:T(4,128)S(1)}, f32[4,64]{1,0:T(4,128)}, u32[]{:S(2)}) copy-start(f32[4,64]{1,0:T(4,128)} %controls.3) | copy-start | bytes 3076
  32.3 2.1 %copy-start.4 = (f32[128]{0:T(128)S(1)}, f32[128]{0:T(128)}, u32[]{:S(2)}) copy-start(f32[128]{0:T(128)} %param.15) | copy-start | bytes 1540
  33.4 4.4 %collective-permute-start.10 = (f32[136,128]{1,0:T(8,128)S(1)}, f32[136,128]{1,0:T(8,128)S(1)}, u32[]{:S(2)}, u32[]{:S(2)}) collective-permute-start(f32[136,128]{1,0:T(8,128)S(1)} %get-tuple-element.29), channel_id=1, source_target_pairs={{0,192},{64,0},{128,64},{192,128},{1,193},{65,1},{129,65},{193,129... | collective-permute-start | bytes 208904 | tf_op jit(solution)/shard_map/ppermute | solution.py:207
  34.4 3.3 %collective-permute-start.9 = (f32[136,128]{1,0:T(8,128)S(1)}, f32[136,128]{1,0:T(8,128)S(1)}, u32[]{:S(2)}, u32[]{:S(2)}) collective-permute-start(f32[136,128]{1,0:T(8,128)S(1)} %collective-permute-done.8.own), channel_id=1, source_target_pairs={{0,1},{1,0},{2,3},{3,2},{4,5},{5,4},{6,7},{7,6},{8,9},{9,8},{10,11... | collective-permute-start | bytes 208904 | tf_op jit(solution)/shard_map/ppermute | solution.py:207

commit v3 on v2

--- a/solution.py
+++ b/solution.py
@@ -118,8 +118,8 @@
     third[...] = joined(half[...], step[...])
 
 
-def pair_kernel(axis, own, other, total):
-    odd = lax.axis_index(axis) % 2 == 1
+def pair_kernel(axes, own, other, total):
+    odd = sum(lax.axis_index(axis) for axis in axes) % 2 == 1
     mine, theirs = own[...], other[...]
     total[...] = compose(jnp.where(odd, theirs, mine), jnp.where(odd, mine, theirs))
 
@@ -136,8 +136,10 @@
     high = place >= 2
     a = own[...]
     behind, c, ahead = arrived(*(ref[...] for ref in refs[:3]))
-    if ring:
+    if ring == 1:
         b, d = jnp.where(odd, behind, ahead), jnp.where(odd, ahead, behind)
+    elif ring == 2:
+        b, d = behind, ahead
     else:
         b, d = ahead, behind
     beside[...] = b
@@ -260,20 +262,26 @@
     def across(value):
         return swap(value, "core", lambda i: i ^ 1)
 
+    def paired(axes, own, other):
+        return call(functools.partial(pair_kernel, axes), square, (own, other), held=(0, 1))
+
+    ring = ([lambda i: (i + 1) % 4, lambda i: (i + 2) % 4], lambda i: (i + 3) % 4)
+
     levels = [("core", 0)]
     other = across(total)
+    back = swap(total, "y", lambda i: i ^ 1)
     earlier = [other]
     upcoming = lead(other)
     settled = core == 0
-    total = call(functools.partial(pair_kernel, "core"), square, (total, other), held=(0, 1))
-
-    def gathered(total, axis, partners, shared, late):
-        def both():
-            return swap(total, axis, shared)
-
-        common = None if late else both()
+    total = paired(("core",), total, other)
+
+    def gathered(total, axis, partners, back=None, axes=None):
         own = apart(total, axis, partners)
-        common = both() if late else common
+        if axes is None:
+            common = swap(total, axis, back)
+        else:
+            other = across(back)
+            common = paired(axes, back, other)
         passed = across(own)
         return own, passed, common
 
@@ -286,26 +294,29 @@
             held=range(4),
         )
         behind, _, ahead = arrived(*map(lead, found))
-        after = ahead if ring else jnp.where(place % 2 == 1, behind, ahead)
+        after = jnp.where(place % 2 == 1, behind, ahead)
+        if ring:
+            after = ahead if ring == 1 else jnp.where(place % 2 == 1, ahead, behind)
         upcoming = jnp.where(settled, upcoming, after)
         settled = jnp.logical_or(settled, place < 3)
         levels.extend([(axis, shift), (axis, shift + 1)])
         earlier.extend([near, others])
         return whole, upcoming, settled
 
-    ring = ([lambda i: (i + 1) % 4, lambda i: (i + 2) % 4], lambda i: (i + 3) % 4)
-    found = gathered(total, "y", *ring, True)
-    total, upcoming, settled = four(total, upcoming, settled, "y", 0, True, found)
+    found = gathered(total, "y", [lambda i: i ^ 3, lambda i: i ^ 2], back, ("core",))
+    total, upcoming, settled = four(total, upcoming, settled, "y", 0, 0, found)
     levels.append(("z", 0))
     other = swap(total, "z", lambda i: i ^ 1)
+    back = apart(total, "z", [lambda i: i ^ 2, lambda i: i ^ 3])
     earlier.append(other)
     upcoming = jnp.where(settled, upcoming, lead(other))
     settled = jnp.logical_or(settled, z % 2 == 0)
-    total = call(functools.partial(pair_kernel, "z"), square, (total, other), held=(0, 1))
-    found = gathered(total, "z", [lambda i: i ^ 6, lambda i: i ^ 5], lambda i: i ^ 2, False)
-    total, upcoming, settled = four(total, upcoming, settled, "z", 1, False, found)
+    total = paired(("z",), total, other)
+    found = gathered(total, "z", [lambda i: i ^ 6, lambda i: i ^ 5], back, ("z", "core"))
+    total, upcoming, settled = four(total, upcoming, settled, "z", 1, 0, found)
     upcoming = jnp.where(jnp.logical_and(~settled, lax.axis_index("seg") == 3), terminal[None], upcoming)
-    found = gathered(total, "seg", [ring[0][0], lambda i: (2, 3, 1, 0)[i]], ring[1], True)
+    partners = [ring[0][0], lambda i: (2, 3, 1, 0)[i]]
+    found = gathered(total, "seg", partners, ring[1])
     before = call(
         functools.partial(before_kernel, levels), square, earlier, held=range(len(earlier))
     )

time: 39.8 us -> 40.2 us (1.010)
  the two profiles are of different devices: /device:TPU:2 before, /device:TPU:1 now
where the time goes in v3:
time: 40.2 us; the launch traced here: 40.1 us
  starting transfers between devices  23 us (57%)
  waiting for transfers between devices  7.62 us (19%)
  Pallas kernels  7.4 us (18%)
  between operations  1.41 us (4%)
  local copies, waits for them, and re-layouts  0.7 us (2%)
    ppermute x4, starting transfers between devices, apart(): return lax.ppermute(value, (axis, 'core'), pairs)  12.3 us
    ppermute x9, starting transfers between devices, swap(): lax.ppermute(value, axis, [(i, partner(i)) for i in range(lax.axis_size(a...  10.7 us
    pallas_call x11, Pallas kernels, call(): pl.pallas_call(kernel, out_shape=shapes, in_specs=[SMEM] * scalars + [VME...  7.4 us
    ppermute x9, waiting for transfers between devices, swap(): lax.ppermute(value, axis, [(i, partner(i)) for i in range(lax.axis_size(a...  4.44 us
    ppermute x4, waiting for transfers between devices, apart(): return lax.ppermute(value, (axis, 'core'), pairs)  3.18 us
  transfers between devices with their start and end apart: 13, of which 7 were waited for; matrix products, arithmetic and copies ran while one was open for 0% of the time, Pallas kernels for 7%

profile of v3, /device:TPU:1, one launch (start us, length us, event | category | flops | bytes accessed | tf_op | source)
XLA Modules:
  0.0 40.1 jit_solution(164471410329811500)
XLA Ops:
  1.3 2.4 %shard_map.104 = (f32[136,128]{1,0:T(8,128)S(1)}, f32[136,128]{1,0:T(8,128)S(1)}, f32[136,128]{1,0:T(8,128)S(1)}, f32[136,128]{1,0:T(8,128)S(1)}, f32[136,128]{1,0:T(8,128)S(1)}) custom-call(s32[1]{0:T(128)S(6)} %copy.11.counts, f32[4,128,128]{2,1,0:T(8,128)} %jacobian.3, f32[4,128,128]{2,1,0:T(8,128)} %inverse.1, f32[4,64,128]{2,1,0:T(8,128)} %bitcast.4, ...), custom_call_target="tpu_custom_call" | custom-call | bytes 400000 | tf_op jit(solution)/shard_map/pallas_call | solution.py:225
  3.6 3.3 %collective-permute-start = (f32[136,128]{1,0:T(8,128)S(1)}, f32[136,128]{1,0:T(8,128)S(1)}, u32[]{:S(2)}, u32[]{:S(2)}) collective-permute-start(f32[136,128]{1,0:T(8,128)S(1)} %get-tuple-element.16.own), channel_id=1, source_target_pairs={{0,1},{1,0},{2,3},{3,2},{4,5},{5,4},{6,7},{7,6},{8,9},{9,8},{10,11... | collective-permute-start | bytes 208904 | tf_op jit(solution)/shard_map/ppermute | solution.py:209
  6.9 0.9 %collective-permute-done.other.refs_0_ = f32[136,128]{1,0:T(8,128)S(1)} collective-permute-done((f32[136,128]{1,0:T(8,128)S(1)}, f32[136,128]{1,0:T(8,128)S(1)}, u32[]{:S(2)}, u32[]{:S(2)}) %collective-permute-start) | collective-permute-done | bytes 69664 | tf_op jit(solution)/shard_map/ppermute | solution.py:209
  7.8 0.2 shard_map.105.own
  8.0 1.4 %collective-permute-start.1 = (f32[136,128]{1,0:T(8,128)S(1)}, f32[136,128]{1,0:T(8,128)S(1)}, u32[]{:S(2)}, u32[]{:S(2)}) collective-permute-start(f32[136,128]{1,0:T(8,128)S(1)} %shard_map.105.own), channel_id=1, source_target_pairs={{0,6},{1,5},{2,4},{3,7},{4,2},{5,1},{6,0},{7,3},{8,14},{9,13},{10,... | collective-permute-start | bytes 208904 | tf_op jit(solution)/shard_map/ppermute | solution.py:260
  9.4 1.1 %collective-permute-done.3.own = f32[136,128]{1,0:T(8,128)S(1)} collective-permute-done((f32[136,128]{1,0:T(8,128)S(1)}, f32[136,128]{1,0:T(8,128)S(1)}, u32[]{:S(2)}, u32[]{:S(2)}) %collective-permute-start.3) | collective-permute-done | bytes 69664 | tf_op jit(solution)/shard_map/ppermute | solution.py:209
  10.6 1.1 %collective-permute-start.4 = (f32[136,128]{1,0:T(8,128)S(1)}, f32[136,128]{1,0:T(8,128)S(1)}, u32[]{:S(2)}, u32[]{:S(2)}) collective-permute-start(f32[136,128]{1,0:T(8,128)S(1)} %collective-permute-done.3.own), channel_id=1, source_target_pairs={{0,1},{1,0},{2,3},{3,2},{4,5},{5,4},{6,7},{7,6},{8,9},{9,8},{10,11... | collective-permute-start | bytes 208904 | tf_op jit(solution)/shard_map/ppermute | solution.py:209
  11.7 1.1 %collective-permute-done.1.refs_0_ = f32[136,128]{1,0:T(8,128)S(1)} collective-permute-done((f32[136,128]{1,0:T(8,128)S(1)}, f32[136,128]{1,0:T(8,128)S(1)}, u32[]{:S(2)}, u32[]{:S(2)}) %collective-permute-start.1) | collective-permute-done | bytes 69664 | tf_op jit(solution)/shard_map/ppermute | solution.py:260
  12.8 1.4 %collective-permute-start.2 = (f32[136,128]{1,0:T(8,128)S(1)}, f32[136,128]{1,0:T(8,128)S(1)}, u32[]{:S(2)}, u32[]{:S(2)}) collective-permute-start(f32[136,128]{1,0:T(8,128)S(1)} %collective-permute-done.1.refs_0_), channel_id=1, source_target_pairs={{0,1},{1,0},{2,3},{3,2},{4,5},{5,4},{6,7},{7,6},{8,9},{9,8},{10,11... | collective-permute-start | bytes 208904 | tf_op jit(solution)/shard_map/ppermute | solution.py:209
  14.2 0.2 shard_map.106.refs_2_
  14.4 0.7 %collective-permute-done.2.refs_1_ = f32[136,128]{1,0:T(8,128)S(1)} collective-permute-done((f32[136,128]{1,0:T(8,128)S(1)}, f32[136,128]{1,0:T(8,128)S(1)}, u32[]{:S(2)}, u32[]{:S(2)}) %collective-permute-start.2) | collective-permute-done | bytes 69664 | tf_op jit(solution)/shard_map/ppermute | solution.py:209
  15.1 0.4 %shard_map.107 = (f32[136,128]{1,0:T(8,128)S(1)}, f32[136,128]{1,0:T(8,128)S(1)}, f32[136,128]{1,0:T(8,128)S(1)}) custom-call(f32[136,128]{1,0:T(8,128)S(1)} %shard_map.105.own, f32[136,128]{1,0:T(8,128)S(1)} %collective-permute-done.1.refs_0_, f32[136,128]{1,0:T(8,128)S(1)} %collective-permute-done.2.refs_1_, f32[136,128]{1,0:T(8,128)S(1)} %shard_map.106.refs_2_), custom_call_target="tpu_custom_call" | custom-call | bytes 400000 | tf_op jit(solution)/shard_map/pallas_call | solution.py:225
  15.5 0.8 %collective-permute-start.5 = (f32[136,128]{1,0:T(8,128)S(1)}, f32[136,128]{1,0:T(8,128)S(1)}, u32[]{:S(2)}, u32[]{:S(2)}) collective-permute-start(f32[136,128]{1,0:T(8,128)S(1)} %get-tuple-element.19.own), channel_id=1, source_target_pairs={{0,8},{8,0},{16,24},{24,16},{32,40},{40,32},{48,56},{56,48},{1,9},... | collective-permute-start | bytes 208904 | tf_op jit(solution)/shard_map/ppermute | solution.py:209
  16.4 2.8 %collective-permute-start.8 = (f32[136,128]{1,0:T(8,128)S(1)}, f32[136,128]{1,0:T(8,128)S(1)}, u32[]{:S(2)}, u32[]{:S(2)}) collective-permute-start(f32[136,128]{1,0:T(8,128)S(1)} %get-tuple-element.19.own), channel_id=1, source_target_pairs={{0,16},{1,25},{8,24},{9,17},{16,0},{17,9},{24,8},{25,1},{32,48},{3... | collective-permute-start | bytes 208904 | tf_op jit(solution)/shard_map/ppermute | solution.py:260
  19.2 0.2 shard_map.108.own
  19.4 5.3 %collective-permute-start.6 = (f32[136,128]{1,0:T(8,128)S(1)}, f32[136,128]{1,0:T(8,128)S(1)}, u32[]{:S(2)}, u32[]{:S(2)}) collective-permute-start(f32[136,128]{1,0:T(8,128)S(1)} %shard_map.108.own), channel_id=1, source_target_pairs={{0,48},{1,41},{8,56},{9,33},{16,32},{17,57},{24,40},{25,49},{32,16... | collective-permute-start | bytes 208904 | tf_op jit(solution)/shard_map/ppermute | solution.py:260
  24.7 1.3 %collective-permute-start.9 = (f32[136,128]{1,0:T(8,128)S(1)}, f32[136,128]{1,0:T(8,128)S(1)}, u32[]{:S(2)}, u32[]{:S(2)}) collective-permute-start(f32[136,128]{1,0:T(8,128)S(1)} %collective-permute-done.8.own), channel_id=1, source_target_pairs={{0,1},{1,0},{2,3},{3,2},{4,5},{5,4},{6,7},{7,6},{8,9},{9,8},{10,11... | collective-permute-start | bytes 208904 | tf_op jit(solution)/shard_map/ppermute | solution.py:209
  26.0 2.1 %collective-permute-done.6.refs_0_ = f32[136,128]{1,0:T(8,128)S(1)} collective-permute-done((f32[136,128]{1,0:T(8,128)S(1)}, f32[136,128]{1,0:T(8,128)S(1)}, u32[]{:S(2)}, u32[]{:S(2)}) %collective-permute-start.6) | collective-permute-done | bytes 69664 | tf_op jit(solution)/shard_map/ppermute | solution.py:260
  28.1 1.3 %collective-permute-start.7 = (f32[136,128]{1,0:T(8,128)S(1)}, f32[136,128]{1,0:T(8,128)S(1)}, u32[]{:S(2)}, u32[]{:S(2)}) collective-permute-start(f32[136,128]{1,0:T(8,128)S(1)} %collective-permute-done.6.refs_0_), channel_id=1, source_target_pairs={{0,1},{1,0},{2,3},{3,2},{4,5},{5,4},{6,7},{7,6},{8,9},{9,8},{10,11... | collective-permute-start | bytes 208904 | tf_op jit(solution)/shard_map/ppermute | solution.py:209
  29.4 0.2 shard_map.109.refs_2_
  29.6 0.7 %collective-permute-done.7.refs_1_ = f32[136,128]{1,0:T(8,128)S(1)} collective-permute-done((f32[136,128]{1,0:T(8,128)S(1)}, f32[136,128]{1,0:T(8,128)S(1)}, u32[]{:S(2)}, u32[]{:S(2)}) %collective-permute-start.7) | collective-permute-done | bytes 69664 | tf_op jit(solution)/shard_map/ppermute | solution.py:209
  30.3 0.4 %shard_map.110 = (f32[136,128]{1,0:T(8,128)S(1)}, f32[136,128]{1,0:T(8,128)S(1)}, f32[136,128]{1,0:T(8,128)S(1)}) custom-call(f32[136,128]{1,0:T(8,128)S(1)} %shard_map.108.own, f32[136,128]{1,0:T(8,128)S(1)} %collective-permute-done.6.refs_0_, f32[136,128]{1,0:T(8,128)S(1)} %collective-permute-done.7.refs_1_, f32[136,128]{1,0:T(8,128)S(1)} %shard_map.109.refs_2_), custom_call_target="tpu_custom_call" | custom-call | bytes 400000 | tf_op jit(solution)/shard_map/pallas_call | solution.py:225
  30.7 2.8 %collective-permute-start.10 = (f32[136,128]{1,0:T(8,128)S(1)}, f32[136,128]{1,0:T(8,128)S(1)}, u32[]{:S(2)}, u32[]{:S(2)}) collective-permute-start(f32[136,128]{1,0:T(8,128)S(1)} %get-tuple-element.29), channel_id=1, source_target_pairs={{0,64},{1,129},{64,128},{65,193},{128,192},{129,65},{192,0},{193,1... | collective-permute-start | bytes 208904 | tf_op jit(solution)/shard_map/ppermute | solution.py:260
  33.6 0.7 %copy-done.3 = f32[4,128]{1,0:T(4,128)S(1)} copy-done((f32[4,128]{1,0:T(4,128)S(1)}, f32[4,128]{1,0:T(4,128)}, u32[]{:S(2)}) %copy-start.3) | copy-done | bytes 2072
  34.2 0.0 copy-done.2
  34.2 1.1 %shard_map.112 = (f32[4,128]{1,0:T(4,128)S(1)}, f32[128,128]{1,0:T(8,128)S(1)}, f32[136,128]{1,0:T(8,128)S(1)}) custom-call(s32[1]{0:T(128)S(6)} %copy.11.counts, f32[4,128,128]{2,1,0:T(8,128)S(1)} %copy-done, f32[4,64,128]{2,1,0:T(8,128)S(1)} %bitcast.5, f32[4,64]{1,0:T(4,128)S(1)} %copy-done.2, f32[4,128]{1,0:T(4,128)S(1)} %copy-done.3, ...), custom_call_target="tpu_custom_call" | custom-call | bytes 400000 | tf_op jit(solution)/shard_map/pallas_call | solution.py:225
  35.3 0.1 collective-permute-start.12
  35.4 1.3 %collective-permute-start.11 = (f32[136,128]{1,0:T(8,128)S(1)}, f32[136,128]{1,0:T(8,128)S(1)}, u32[]{:S(2)}, u32[]{:S(2)}) collective-permute-start(f32[136,128]{1,0:T(8,128)S(1)} %collective-permute-done.10.own), channel_id=1, source_target_pairs={{0,1},{1,0},{2,3},{3,2},{4,5},{5,4},{6,7},{7,6},{8,9},{9,8},{10,11... | collective-permute-start | bytes 208904 | tf_op jit(solution)/shard_map/ppermute | solution.py:209
  36.7 0.9 %shard_map.111.before = f32[136,128]{1,0:T(8,128)S(1)} custom-call(f32[136,128]{1,0:T(8,128)S(1)} %collective-permute-done.other.refs_0_, f32[136,128]{1,0:T(8,128)S(1)} %get-tuple-element.17.refs_1_, f32[136,128]{1,0:T(8,128)S(1)} %get-tuple-element.18.refs_2_, f32[136,128]{1,0:T(8,128)S(1)} %collective-permute-done.5.other.refs_3_, ...), custom_call_target="tpu_custom_call" | custom-call | bytes 400000 | tf_op jit(solution)/shard_map/pallas_call | solution.py:225
  37.6 0.3 shard_map.113.reach
  37.9 1.0 %collective-permute-done.12.common = f32[136,128]{1,0:T(8,128)S(1)} collective-permute-done((f32[136,128]{1,0:T(8,128)S(1)}, f32[136,128]{1,0:T(8,128)S(1)}, u32[]{:S(2)}, u32[]{:S(2)}) %collective-permute-start.12) | collective-permute-done | bytes 69664 | tf_op jit(solution)/shard_map/ppermute | solution.py:209
  38.9 1.2 %shard_map.114 = (f32[4,128]{1,0:T(4,128)}, f32[4,128]{1,0:T(4,128)}) custom-call(s32[1]{0:T(128)S(6)} %copy.11.counts, f32[4,136,128]{2,1,0:T(8,128)S(1)} %shard_map.113.reach, f32[1,128]{1,0:T(1,128)S(1)} %broadcast_select_fusion.7.upcoming, f32[4,128]{1,0:T(4,128)S(1)} %get-tuple-element.27.base, f32[128,128]{1,0:T(8,128)S(1)} %get-tuple-element.28.last, ...), custom_call_target="tpu_custom_call" | custom-call | bytes 400000 | tf_op jit(solution)/shard_map/pallas_call | solution.py:225
  (16 shorter events, 0.0 us)
Async XLA Ops:
  3.6 4.2 %collective-permute-start = (f32[136,128]{1,0:T(8,128)S(1)}, f32[136,128]{1,0:T(8,128)S(1)}, u32[]{:S(2)}, u32[]{:S(2)}) collective-permute-start(f32[136,128]{1,0:T(8,128)S(1)} %get-tuple-element.16.own), channel_id=1, source_target_pairs={{0,1},{1,0},{2,3},{3,2},{4,5},{5,4},{6,7},{7,6},{8,9},{9,8},{10,11... | collective-permute-start | bytes 208904 | tf_op jit(solution)/shard_map/ppermute | solution.py:209
  6.9 3.6 %collective-permute-start.3 = (f32[136,128]{1,0:T(8,128)S(1)}, f32[136,128]{1,0:T(8,128)S(1)}, u32[]{:S(2)}, u32[]{:S(2)}) collective-permute-start(f32[136,128]{1,0:T(8,128)S(1)} %get-tuple-element.16.own), channel_id=1, source_target_pairs={{0,2},{2,0},{4,6},{6,4},{1,3},{3,1},{5,7},{7,5},{8,10},{10,8},{12,... | collective-permute-start | bytes 208904 | tf_op jit(solution)/shard_map/ppermute | solution.py:209
  8.0 4.8 %collective-permute-start.1 = (f32[136,128]{1,0:T(8,128)S(1)}, f32[136,128]{1,0:T(8,128)S(1)}, u32[]{:S(2)}, u32[]{:S(2)}) collective-permute-start(f32[136,128]{1,0:T(8,128)S(1)} %shard_map.105.own), channel_id=1, source_target_pairs={{0,6},{1,5},{2,4},{3,7},{4,2},{5,1},{6,0},{7,3},{8,14},{9,13},{10,... | collective-permute-start | bytes 208904 | tf_op jit(solution)/shard_map/ppermute | solution.py:260
  10.6 3.7 %collective-permute-start.4 = (f32[136,128]{1,0:T(8,128)S(1)}, f32[136,128]{1,0:T(8,128)S(1)}, u32[]{:S(2)}, u32[]{:S(2)}) collective-permute-start(f32[136,128]{1,0:T(8,128)S(1)} %collective-permute-done.3.own), channel_id=1, source_target_pairs={{0,1},{1,0},{2,3},{3,2},{4,5},{5,4},{6,7},{7,6},{8,9},{9,8},{10,11... | collective-permute-start | bytes 208904 | tf_op jit(solution)/shard_map/ppermute | solution.py:209
  12.8 2.3 %collective-permute-start.2 = (f32[136,128]{1,0:T(8,128)S(1)}, f32[136,128]{1,0:T(8,128)S(1)}, u32[]{:S(2)}, u32[]{:S(2)}) collective-permute-start(f32[136,128]{1,0:T(8,128)S(1)} %collective-permute-done.1.refs_0_), channel_id=1, source_target_pairs={{0,1},{1,0},{2,3},{3,2},{4,5},{5,4},{6,7},{7,6},{8,9},{9,8},{10,11... | collective-permute-start | bytes 208904 | tf_op jit(solution)/shard_map/ppermute | solution.py:209
  15.5 3.6 %collective-permute-start.5 = (f32[136,128]{1,0:T(8,128)S(1)}, f32[136,128]{1,0:T(8,128)S(1)}, u32[]{:S(2)}, u32[]{:S(2)}) collective-permute-start(f32[136,128]{1,0:T(8,128)S(1)} %get-tuple-element.19.own), channel_id=1, source_target_pairs={{0,8},{8,0},{16,24},{24,16},{32,40},{40,32},{48,56},{56,48},{1,9},... | collective-permute-start | bytes 208904 | tf_op jit(solution)/shard_map/ppermute | solution.py:209
  16.4 8.3 %collective-permute-start.8 = (f32[136,128]{1,0:T(8,128)S(1)}, f32[136,128]{1,0:T(8,128)S(1)}, u32[]{:S(2)}, u32[]{:S(2)}) collective-permute-start(f32[136,128]{1,0:T(8,128)S(1)} %get-tuple-element.19.own), channel_id=1, source_target_pairs={{0,16},{1,25},{8,24},{9,17},{16,0},{17,9},{24,8},{25,1},{32,48},{3... | collective-permute-start | bytes 208904 | tf_op jit(solution)/shard_map/ppermute | solution.py:260
  19.4 14.2 %copy-start = (f32[4,128,128]{2,1,0:T(8,128)S(1)}, f32[4,128,128]{2,1,0:T(8,128)}, u32[]{:S(2)}) copy-start(f32[4,128,128]{2,1,0:T(8,128)} %jacobian.3) | copy-start | bytes 786436
  19.4 8.7 %collective-permute-start.6 = (f32[136,128]{1,0:T(8,128)S(1)}, f32[136,128]{1,0:T(8,128)S(1)}, u32[]{:S(2)}, u32[]{:S(2)}) collective-permute-start(f32[136,128]{1,0:T(8,128)S(1)} %shard_map.108.own), channel_id=1, source_target_pairs={{0,48},{1,41},{8,56},{9,33},{16,32},{17,57},{24,40},{25,49},{32,16... | collective-permute-start | bytes 208904 | tf_op jit(solution)/shard_map/ppermute | solution.py:260
  24.7 4.7 %collective-permute-start.9 = (f32[136,128]{1,0:T(8,128)S(1)}, f32[136,128]{1,0:T(8,128)S(1)}, u32[]{:S(2)}, u32[]{:S(2)}) collective-permute-start(f32[136,128]{1,0:T(8,128)S(1)} %collective-permute-done.8.own), channel_id=1, source_target_pairs={{0,1},{1,0},{2,3},{3,2},{4,5},{5,4},{6,7},{7,6},{8,9},{9,8},{10,11... | collective-permute-start | bytes 208904 | tf_op jit(solution)/shard_map/ppermute | solution.py:209
  28.1 2.2 %collective-permute-start.7 = (f32[136,128]{1,0:T(8,128)S(1)}, f32[136,128]{1,0:T(8,128)S(1)}, u32[]{:S(2)}, u32[]{:S(2)}) collective-permute-start(f32[136,128]{1,0:T(8,128)S(1)} %collective-permute-done.6.refs_0_), channel_id=1, source_target_pairs={{0,1},{1,0},{2,3},{3,2},{4,5},{5,4},{6,7},{7,6},{8,9},{9,8},{10,11... | collective-permute-start | bytes 208904 | tf_op jit(solution)/shard_map/ppermute | solution.py:209
  29.6 3.9 %copy-start.1 = (f32[4,128,64]{1,2,0:T(8,128)S(1)}, f32[4,128,64]{1,2,0:T(8,128)}, u32[]{:S(2)}) copy-start(f32[4,128,64]{1,2,0:T(8,128)} %param.11) | copy-start | bytes 393220
  30.7 4.7 %collective-permute-start.10 = (f32[136,128]{1,0:T(8,128)S(1)}, f32[136,128]{1,0:T(8,128)S(1)}, u32[]{:S(2)}, u32[]{:S(2)}) collective-permute-start(f32[136,128]{1,0:T(8,128)S(1)} %get-tuple-element.29), channel_id=1, source_target_pairs={{0,64},{1,129},{64,128},{65,193},{128,192},{129,65},{192,0},{193,1... | collective-permute-start | bytes 208904 | tf_op jit(solution)/shard_map/ppermute | solution.py:260
  33.5 0.7 %copy-start.3 = (f32[4,128]{1,0:T(4,128)S(1)}, f32[4,128]{1,0:T(4,128)}, u32[]{:S(2)}) copy-start(f32[4,128]{1,0:T(4,128)} %states.3) | copy-start | bytes 6148
  33.5 0.7 %copy-start.2 = (f32[4,64]{1,0:T(4,128)S(1)}, f32[4,64]{1,0:T(4,128)}, u32[]{:S(2)}) copy-start(f32[4,64]{1,0:T(4,128)} %controls.3) | copy-start | bytes 3076
  34.2 2.4 %copy-start.4 = (f32[128]{0:T(128)S(1)}, f32[128]{0:T(128)}, u32[]{:S(2)}) copy-start(f32[128]{0:T(128)} %param.15) | copy-start | bytes 1540
  35.3 3.5 %collective-permute-start.12 = (f32[136,128]{1,0:T(8,128)S(1)}, f32[136,128]{1,0:T(8,128)S(1)}, u32[]{:S(2)}, u32[]{:S(2)}) collective-permute-start(f32[136,128]{1,0:T(8,128)S(1)} %get-tuple-element.29), channel_id=1, source_target_pairs={{0,192},{64,0},{128,64},{192,128},{1,193},{65,1},{129,65},{193,129... | collective-permute-start | bytes 208904 | tf_op jit(solution)/shard_map/ppermute | solution.py:209
  35.4 3.4 %collective-permute-start.11 = (f32[136,128]{1,0:T(8,128)S(1)}, f32[136,128]{1,0:T(8,128)S(1)}, u32[]{:S(2)}, u32[]{:S(2)}) collective-permute-start(f32[136,128]{1,0:T(8,128)S(1)} %collective-permute-done.10.own), channel_id=1, source_target_pairs={{0,1},{1,0},{2,3},{3,2},{4,5},{5,4},{6,7},{7,6},{8,9},{9,8},{10,11... | collective-permute-start | bytes 208904 | tf_op jit(solution)/shard_map/ppermute | solution.py:209

commit v4 on v3

--- a/solution.py
+++ b/solution.py
@@ -182,7 +182,8 @@
     def moved(start, way):
         return product(parts(wide(start)), parts(way[:width]))[0:1] + way[width : width + 1]
 
-    start = jnp.where(x == 3, ahead, jnp.where(x == 2, back2, back))[width : width + 1]
+    start = jnp.where(x == 2, back2, back)[width : width + 1]
+    start = jnp.where(x == 3, ahead[0:1], start)
     start = jnp.where(x == 0, 0.0, start)
     start = jnp.where(x >= 2, moved(start, jnp.where(x == 3, back2, back)), start)
     start = jnp.where(x == 3, moved(start, back), start)
@@ -196,7 +197,7 @@
             jnp.logical_and(lax.axis_index("y") == 3, lax.axis_index("core") == 1),
         )
     )
-    after = ahead[width + 1 : width + 2]
+    after = ahead[1:2]
     after = jnp.where(jnp.logical_or(settled, x == 3), upcoming[...], after)
     matrix = parts(last[...])
     once = product(parts(wide(after)), matrix, NT)
@@ -278,7 +279,7 @@
     def gathered(total, axis, partners, back=None, axes=None):
         own = apart(total, axis, partners)
         if axes is None:
-            common = swap(total, axis, back)
+            common = swap(total[width:], axis, back)
         else:
             other = across(back)
             common = paired(axes, back, other)

time: 40.2 us -> 39.3 us (0.978)
  waiting for transfers between devices: 7.62 us -> 6.64 us
    ppermute x9, waiting for transfers between devices: 4.44 us -> 3.46 us  [swap(): lax.ppermute(value, axis, [(i, partner(i)) for i in range(lax.axis_size(a...]
  transfers between devices with their start and end apart: 13 -> 13, of which waited for: 7 -> 6; matrix products, arithmetic and copies ran while one was open for 0% -> 0% of each run, Pallas kernels for 7% -> 8%
where the time goes in v4:
time: 39.3 us; the launch traced here: 39.1 us
  starting transfers between devices  22.9 us (58%)
  Pallas kernels  7.41 us (19%)
  waiting for transfers between devices  6.64 us (17%)
  between operations  1.44 us (4%)
  local copies, waits for them, and re-layouts  0.71 us (2%)
    ppermute x4, starting transfers between devices, apart(): return lax.ppermute(value, (axis, 'core'), pairs)  12.3 us
    ppermute x9, starting transfers between devices, swap(): lax.ppermute(value, axis, [(i, partner(i)) for i in range(lax.axis_size(a...  10.7 us
    pallas_call x11, Pallas kernels, call(): pl.pallas_call(kernel, out_shape=shapes, in_specs=[SMEM] * scalars + [VME...  7.41 us
    ppermute x9, waiting for transfers between devices, swap(): lax.ppermute(value, axis, [(i, partner(i)) for i in range(lax.axis_size(a...  3.46 us
    ppermute x4, waiting for transfers between devices, apart(): return lax.ppermute(value, (axis, 'core'), pairs)  3.18 us
  transfers between devices with their start and end apart: 13, of which 6 were waited for; matrix products, arithmetic and copies ran while one was open for 0% of the time, Pallas kernels for 8%

profile of v4, /device:TPU:1, one launch (start us, length us, event | category | flops | bytes accessed | tf_op | source)
XLA Modules:
  0.0 39.1 jit_solution(17721304289844406654)
XLA Ops:
  1.3 2.4 %shard_map.104 = (f32[136,128]{1,0:T(8,128)S(1)}, f32[136,128]{1,0:T(8,128)S(1)}, f32[136,128]{1,0:T(8,128)S(1)}, f32[136,128]{1,0:T(8,128)S(1)}, f32[136,128]{1,0:T(8,128)S(1)}) custom-call(s32[1]{0:T(128)S(6)} %copy.11.counts, f32[4,128,128]{2,1,0:T(8,128)} %jacobian.3, f32[4,128,128]{2,1,0:T(8,128)} %inverse.1, f32[4,64,128]{2,1,0:T(8,128)} %bitcast.4, ...), custom_call_target="tpu_custom_call" | custom-call | bytes 400000 | tf_op jit(solution)/shard_map/pallas_call | solution.py:226
  3.6 3.3 %collective-permute-start = (f32[136,128]{1,0:T(8,128)S(1)}, f32[136,128]{1,0:T(8,128)S(1)}, u32[]{:S(2)}, u32[]{:S(2)}) collective-permute-start(f32[136,128]{1,0:T(8,128)S(1)} %get-tuple-element.16.own), channel_id=1, source_target_pairs={{0,1},{1,0},{2,3},{3,2},{4,5},{5,4},{6,7},{7,6},{8,9},{9,8},{10,11... | collective-permute-start | bytes 208904 | tf_op jit(solution)/shard_map/ppermute | solution.py:210
  6.9 0.9 %collective-permute-done.other.refs_0_ = f32[136,128]{1,0:T(8,128)S(1)} collective-permute-done((f32[136,128]{1,0:T(8,128)S(1)}, f32[136,128]{1,0:T(8,128)S(1)}, u32[]{:S(2)}, u32[]{:S(2)}) %collective-permute-start) | collective-permute-done | bytes 69664 | tf_op jit(solution)/shard_map/ppermute | solution.py:210
  7.8 0.2 shard_map.105.own
  8.0 1.4 %collective-permute-start.1 = (f32[136,128]{1,0:T(8,128)S(1)}, f32[136,128]{1,0:T(8,128)S(1)}, u32[]{:S(2)}, u32[]{:S(2)}) collective-permute-start(f32[136,128]{1,0:T(8,128)S(1)} %shard_map.105.own), channel_id=1, source_target_pairs={{0,6},{1,5},{2,4},{3,7},{4,2},{5,1},{6,0},{7,3},{8,14},{9,13},{10,... | collective-permute-start | bytes 208904 | tf_op jit(solution)/shard_map/ppermute | solution.py:261
  9.4 1.1 %collective-permute-done.3.own = f32[136,128]{1,0:T(8,128)S(1)} collective-permute-done((f32[136,128]{1,0:T(8,128)S(1)}, f32[136,128]{1,0:T(8,128)S(1)}, u32[]{:S(2)}, u32[]{:S(2)}) %collective-permute-start.3) | collective-permute-done | bytes 69664 | tf_op jit(solution)/shard_map/ppermute | solution.py:210
  10.6 1.1 %collective-permute-start.4 = (f32[136,128]{1,0:T(8,128)S(1)}, f32[136,128]{1,0:T(8,128)S(1)}, u32[]{:S(2)}, u32[]{:S(2)}) collective-permute-start(f32[136,128]{1,0:T(8,128)S(1)} %collective-permute-done.3.own), channel_id=1, source_target_pairs={{0,1},{1,0},{2,3},{3,2},{4,5},{5,4},{6,7},{7,6},{8,9},{9,8},{10,11... | collective-permute-start | bytes 208904 | tf_op jit(solution)/shard_map/ppermute | solution.py:210
  11.7 1.1 %collective-permute-done.1.refs_0_ = f32[136,128]{1,0:T(8,128)S(1)} collective-permute-done((f32[136,128]{1,0:T(8,128)S(1)}, f32[136,128]{1,0:T(8,128)S(1)}, u32[]{:S(2)}, u32[]{:S(2)}) %collective-permute-start.1) | collective-permute-done | bytes 69664 | tf_op jit(solution)/shard_map/ppermute | solution.py:261
  12.8 1.4 %collective-permute-start.2 = (f32[136,128]{1,0:T(8,128)S(1)}, f32[136,128]{1,0:T(8,128)S(1)}, u32[]{:S(2)}, u32[]{:S(2)}) collective-permute-start(f32[136,128]{1,0:T(8,128)S(1)} %collective-permute-done.1.refs_0_), channel_id=1, source_target_pairs={{0,1},{1,0},{2,3},{3,2},{4,5},{5,4},{6,7},{7,6},{8,9},{9,8},{10,11... | collective-permute-start | bytes 208904 | tf_op jit(solution)/shard_map/ppermute | solution.py:210
  14.2 0.2 shard_map.106.refs_2_
  14.4 0.7 %collective-permute-done.2.refs_1_ = f32[136,128]{1,0:T(8,128)S(1)} collective-permute-done((f32[136,128]{1,0:T(8,128)S(1)}, f32[136,128]{1,0:T(8,128)S(1)}, u32[]{:S(2)}, u32[]{:S(2)}) %collective-permute-start.2) | collective-permute-done | bytes 69664 | tf_op jit(solution)/shard_map/ppermute | solution.py:210
  15.1 0.4 %shard_map.107 = (f32[136,128]{1,0:T(8,128)S(1)}, f32[136,128]{1,0:T(8,128)S(1)}, f32[136,128]{1,0:T(8,128)S(1)}) custom-call(f32[136,128]{1,0:T(8,128)S(1)} %shard_map.105.own, f32[136,128]{1,0:T(8,128)S(1)} %collective-permute-done.1.refs_0_, f32[136,128]{1,0:T(8,128)S(1)} %collective-permute-done.2.refs_1_, f32[136,128]{1,0:T(8,128)S(1)} %shard_map.106.refs_2_), custom_call_target="tpu_custom_call" | custom-call | bytes 400000 | tf_op jit(solution)/shard_map/pallas_call | solution.py:226
  15.5 0.8 %collective-permute-start.5 = (f32[136,128]{1,0:T(8,128)S(1)}, f32[136,128]{1,0:T(8,128)S(1)}, u32[]{:S(2)}, u32[]{:S(2)}) collective-permute-start(f32[136,128]{1,0:T(8,128)S(1)} %get-tuple-element.19.own), channel_id=1, source_target_pairs={{0,8},{8,0},{16,24},{24,16},{32,40},{40,32},{48,56},{56,48},{1,9},... | collective-permute-start | bytes 208904 | tf_op jit(solution)/shard_map/ppermute | solution.py:210
  16.4 2.8 %collective-permute-start.8 = (f32[136,128]{1,0:T(8,128)S(1)}, f32[136,128]{1,0:T(8,128)S(1)}, u32[]{:S(2)}, u32[]{:S(2)}) collective-permute-start(f32[136,128]{1,0:T(8,128)S(1)} %get-tuple-element.19.own), channel_id=1, source_target_pairs={{0,16},{1,25},{8,24},{9,17},{16,0},{17,9},{24,8},{25,1},{32,48},{3... | collective-permute-start | bytes 208904 | tf_op jit(solution)/shard_map/ppermute | solution.py:261
  19.2 0.2 shard_map.108.own
  19.4 5.3 %collective-permute-start.6 = (f32[136,128]{1,0:T(8,128)S(1)}, f32[136,128]{1,0:T(8,128)S(1)}, u32[]{:S(2)}, u32[]{:S(2)}) collective-permute-start(f32[136,128]{1,0:T(8,128)S(1)} %shard_map.108.own), channel_id=1, source_target_pairs={{0,48},{1,41},{8,56},{9,33},{16,32},{17,57},{24,40},{25,49},{32,16... | collective-permute-start | bytes 208904 | tf_op jit(solution)/shard_map/ppermute | solution.py:261
  24.7 1.3 %collective-permute-start.9 = (f32[136,128]{1,0:T(8,128)S(1)}, f32[136,128]{1,0:T(8,128)S(1)}, u32[]{:S(2)}, u32[]{:S(2)}) collective-permute-start(f32[136,128]{1,0:T(8,128)S(1)} %collective-permute-done.8.own), channel_id=1, source_target_pairs={{0,1},{1,0},{2,3},{3,2},{4,5},{5,4},{6,7},{7,6},{8,9},{9,8},{10,11... | collective-permute-start | bytes 208904 | tf_op jit(solution)/shard_map/ppermute | solution.py:210
  26.0 2.1 %collective-permute-done.6.refs_0_ = f32[136,128]{1,0:T(8,128)S(1)} collective-permute-done((f32[136,128]{1,0:T(8,128)S(1)}, f32[136,128]{1,0:T(8,128)S(1)}, u32[]{:S(2)}, u32[]{:S(2)}) %collective-permute-start.6) | collective-permute-done | bytes 69664 | tf_op jit(solution)/shard_map/ppermute | solution.py:261
  28.1 1.3 %collective-permute-start.7 = (f32[136,128]{1,0:T(8,128)S(1)}, f32[136,128]{1,0:T(8,128)S(1)}, u32[]{:S(2)}, u32[]{:S(2)}) collective-permute-start(f32[136,128]{1,0:T(8,128)S(1)} %collective-permute-done.6.refs_0_), channel_id=1, source_target_pairs={{0,1},{1,0},{2,3},{3,2},{4,5},{5,4},{6,7},{7,6},{8,9},{9,8},{10,11... | collective-permute-start | bytes 208904 | tf_op jit(solution)/shard_map/ppermute | solution.py:210
  29.4 0.2 shard_map.109.refs_2_
  29.6 0.0 copy-start.1
  29.6 0.7 %collective-permute-done.7.refs_1_ = f32[136,128]{1,0:T(8,128)S(1)} collective-permute-done((f32[136,128]{1,0:T(8,128)S(1)}, f32[136,128]{1,0:T(8,128)S(1)}, u32[]{:S(2)}, u32[]{:S(2)}) %collective-permute-start.7) | collective-permute-done | bytes 69664 | tf_op jit(solution)/shard_map/ppermute | solution.py:210
  30.3 0.4 %shard_map.110 = (f32[136,128]{1,0:T(8,128)S(1)}, f32[136,128]{1,0:T(8,128)S(1)}, f32[136,128]{1,0:T(8,128)S(1)}) custom-call(f32[136,128]{1,0:T(8,128)S(1)} %shard_map.108.own, f32[136,128]{1,0:T(8,128)S(1)} %collective-permute-done.6.refs_0_, f32[136,128]{1,0:T(8,128)S(1)} %collective-permute-done.7.refs_1_, f32[136,128]{1,0:T(8,128)S(1)} %shard_map.109.refs_2_), custom_call_target="tpu_custom_call" | custom-call | bytes 400000 | tf_op jit(solution)/shard_map/pallas_call | solution.py:226
  30.7 2.8 %collective-permute-start.10 = (f32[136,128]{1,0:T(8,128)S(1)}, f32[136,128]{1,0:T(8,128)S(1)}, u32[]{:S(2)}, u32[]{:S(2)}) collective-permute-start(f32[136,128]{1,0:T(8,128)S(1)} %get-tuple-element.29), channel_id=1, source_target_pairs={{0,64},{1,129},{64,128},{65,193},{128,192},{129,65},{192,0},{193,1... | collective-permute-start | bytes 208904 | tf_op jit(solution)/shard_map/ppermute | solution.py:261
  33.6 0.7 %copy-done.3 = f32[4,128]{1,0:T(4,128)S(1)} copy-done((f32[4,128]{1,0:T(4,128)S(1)}, f32[4,128]{1,0:T(4,128)}, u32[]{:S(2)}) %copy-start.3) | copy-done | bytes 2072
  34.2 0.0 copy-done.2
  34.2 1.1 %shard_map.112 = (f32[4,128]{1,0:T(4,128)S(1)}, f32[128,128]{1,0:T(8,128)S(1)}, f32[136,128]{1,0:T(8,128)S(1)}) custom-call(s32[1]{0:T(128)S(6)} %copy.11.counts, f32[4,128,128]{2,1,0:T(8,128)S(1)} %copy-done, f32[4,64,128]{2,1,0:T(8,128)S(1)} %bitcast.5, f32[4,64]{1,0:T(4,128)S(1)} %copy-done.2, f32[4,128]{1,0:T(4,128)S(1)} %copy-done.3, ...), custom_call_target="tpu_custom_call" | custom-call | bytes 400000 | tf_op jit(solution)/shard_map/pallas_call | solution.py:226
  35.3 0.1 collective-permute-start.12
  35.4 1.2 %collective-permute-start.11 = (f32[136,128]{1,0:T(8,128)S(1)}, f32[136,128]{1,0:T(8,128)S(1)}, u32[]{:S(2)}, u32[]{:S(2)}) collective-permute-start(f32[136,128]{1,0:T(8,128)S(1)} %collective-permute-done.10.own), channel_id=1, source_target_pairs={{0,1},{1,0},{2,3},{3,2},{4,5},{5,4},{6,7},{7,6},{8,9},{9,8},{10,11... | collective-permute-start | bytes 208904 | tf_op jit(solution)/shard_map/ppermute | solution.py:210
  36.7 0.9 %shard_map.111.before = f32[136,128]{1,0:T(8,128)S(1)} custom-call(f32[136,128]{1,0:T(8,128)S(1)} %collective-permute-done.other.refs_0_, f32[136,128]{1,0:T(8,128)S(1)} %get-tuple-element.17.refs_1_, f32[136,128]{1,0:T(8,128)S(1)} %get-tuple-element.18.refs_2_, f32[136,128]{1,0:T(8,128)S(1)} %collective-permute-done.5.other.refs_3_, ...), custom_call_target="tpu_custom_call" | custom-call | bytes 400000 | tf_op jit(solution)/shard_map/pallas_call | solution.py:226
  37.6 0.3 shard_map.113.reach
  37.9 1.3 %shard_map.114 = (f32[4,128]{1,0:T(4,128)}, f32[4,128]{1,0:T(4,128)}) custom-call(s32[1]{0:T(128)S(6)} %copy.11.counts, f32[4,136,128]{2,1,0:T(8,128)S(1)} %shard_map.113.reach, f32[1,128]{1,0:T(1,128)S(1)} %broadcast_select_fusion.7.upcoming, f32[4,128]{1,0:T(4,128)S(1)} %get-tuple-element.27.base, f32[128,128]{1,0:T(8,128)S(1)} %get-tuple-element.28.last, ...), custom_call_target="tpu_custom_call" | custom-call | bytes 400000 | tf_op jit(solution)/shard_map/pallas_call | solution.py:226
  (17 shorter events, 0.1 us)
Async XLA Ops:
  3.6 4.2 %collective-permute-start = (f32[136,128]{1,0:T(8,128)S(1)}, f32[136,128]{1,0:T(8,128)S(1)}, u32[]{:S(2)}, u32[]{:S(2)}) collective-permute-start(f32[136,128]{1,0:T(8,128)S(1)} %get-tuple-element.16.own), channel_id=1, source_target_pairs={{0,1},{1,0},{2,3},{3,2},{4,5},{5,4},{6,7},{7,6},{8,9},{9,8},{10,11... | collective-permute-start | bytes 208904 | tf_op jit(solution)/shard_map/ppermute | solution.py:210
  6.9 3.6 %collective-permute-start.3 = (f32[136,128]{1,0:T(8,128)S(1)}, f32[136,128]{1,0:T(8,128)S(1)}, u32[]{:S(2)}, u32[]{:S(2)}) collective-permute-start(f32[136,128]{1,0:T(8,128)S(1)} %get-tuple-element.16.own), channel_id=1, source_target_pairs={{0,2},{2,0},{4,6},{6,4},{1,3},{3,1},{5,7},{7,5},{8,10},{10,8},{12,... | collective-permute-start | bytes 208904 | tf_op jit(solution)/shard_map/ppermute | solution.py:210
  8.0 4.8 %collective-permute-start.1 = (f32[136,128]{1,0:T(8,128)S(1)}, f32[136,128]{1,0:T(8,128)S(1)}, u32[]{:S(2)}, u32[]{:S(2)}) collective-permute-start(f32[136,128]{1,0:T(8,128)S(1)} %shard_map.105.own), channel_id=1, source_target_pairs={{0,6},{1,5},{2,4},{3,7},{4,2},{5,1},{6,0},{7,3},{8,14},{9,13},{10,... | collective-permute-start | bytes 208904 | tf_op jit(solution)/shard_map/ppermute | solution.py:261
  10.6 3.7 %collective-permute-start.4 = (f32[136,128]{1,0:T(8,128)S(1)}, f32[136,128]{1,0:T(8,128)S(1)}, u32[]{:S(2)}, u32[]{:S(2)}) collective-permute-start(f32[136,128]{1,0:T(8,128)S(1)} %collective-permute-done.3.own), channel_id=1, source_target_pairs={{0,1},{1,0},{2,3},{3,2},{4,5},{5,4},{6,7},{7,6},{8,9},{9,8},{10,11... | collective-permute-start | bytes 208904 | tf_op jit(solution)/shard_map/ppermute | solution.py:210
  12.8 2.3 %collective-permute-start.2 = (f32[136,128]{1,0:T(8,128)S(1)}, f32[136,128]{1,0:T(8,128)S(1)}, u32[]{:S(2)}, u32[]{:S(2)}) collective-permute-start(f32[136,128]{1,0:T(8,128)S(1)} %collective-permute-done.1.refs_0_), channel_id=1, source_target_pairs={{0,1},{1,0},{2,3},{3,2},{4,5},{5,4},{6,7},{7,6},{8,9},{9,8},{10,11... | collective-permute-start | bytes 208904 | tf_op jit(solution)/shard_map/ppermute | solution.py:210
  15.5 3.6 %collective-permute-start.5 = (f32[136,128]{1,0:T(8,128)S(1)}, f32[136,128]{1,0:T(8,128)S(1)}, u32[]{:S(2)}, u32[]{:S(2)}) collective-permute-start(f32[136,128]{1,0:T(8,128)S(1)} %get-tuple-element.19.own), channel_id=1, source_target_pairs={{0,8},{8,0},{16,24},{24,16},{32,40},{40,32},{48,56},{56,48},{1,9},... | collective-permute-start | bytes 208904 | tf_op jit(solution)/shard_map/ppermute | solution.py:210
  16.4 8.3 %collective-permute-start.8 = (f32[136,128]{1,0:T(8,128)S(1)}, f32[136,128]{1,0:T(8,128)S(1)}, u32[]{:S(2)}, u32[]{:S(2)}) collective-permute-start(f32[136,128]{1,0:T(8,128)S(1)} %get-tuple-element.19.own), channel_id=1, source_target_pairs={{0,16},{1,25},{8,24},{9,17},{16,0},{17,9},{24,8},{25,1},{32,48},{3... | collective-permute-start | bytes 208904 | tf_op jit(solution)/shard_map/ppermute | solution.py:261
  19.4 14.2 %copy-start = (f32[4,128,128]{2,1,0:T(8,128)S(1)}, f32[4,128,128]{2,1,0:T(8,128)}, u32[]{:S(2)}) copy-start(f32[4,128,128]{2,1,0:T(8,128)} %jacobian.3) | copy-start | bytes 786436
  19.4 8.7 %collective-permute-start.6 = (f32[136,128]{1,0:T(8,128)S(1)}, f32[136,128]{1,0:T(8,128)S(1)}, u32[]{:S(2)}, u32[]{:S(2)}) collective-permute-start(f32[136,128]{1,0:T(8,128)S(1)} %shard_map.108.own), channel_id=1, source_target_pairs={{0,48},{1,41},{8,56},{9,33},{16,32},{17,57},{24,40},{25,49},{32,16... | collective-permute-start | bytes 208904 | tf_op jit(solution)/shard_map/ppermute | solution.py:261
  24.7 4.7 %collective-permute-start.9 = (f32[136,128]{1,0:T(8,128)S(1)}, f32[136,128]{1,0:T(8,128)S(1)}, u32[]{:S(2)}, u32[]{:S(2)}) collective-permute-start(f32[136,128]{1,0:T(8,128)S(1)} %collective-permute-done.8.own), channel_id=1, source_target_pairs={{0,1},{1,0},{2,3},{3,2},{4,5},{5,4},{6,7},{7,6},{8,9},{9,8},{10,11... | collective-permute-start | bytes 208904 | tf_op jit(solution)/shard_map/ppermute | solution.py:210
  28.1 2.2 %collective-permute-start.7 = (f32[136,128]{1,0:T(8,128)S(1)}, f32[136,128]{1,0:T(8,128)S(1)}, u32[]{:S(2)}, u32[]{:S(2)}) collective-permute-start(f32[136,128]{1,0:T(8,128)S(1)} %collective-permute-done.6.refs_0_), channel_id=1, source_target_pairs={{0,1},{1,0},{2,3},{3,2},{4,5},{5,4},{6,7},{7,6},{8,9},{9,8},{10,11... | collective-permute-start | bytes 208904 | tf_op jit(solution)/shard_map/ppermute | solution.py:210
  29.6 3.9 %copy-start.1 = (f32[4,128,64]{1,2,0:T(8,128)S(1)}, f32[4,128,64]{1,2,0:T(8,128)}, u32[]{:S(2)}) copy-start(f32[4,128,64]{1,2,0:T(8,128)} %param.11) | copy-start | bytes 393220
  30.7 4.7 %collective-permute-start.10 = (f32[136,128]{1,0:T(8,128)S(1)}, f32[136,128]{1,0:T(8,128)S(1)}, u32[]{:S(2)}, u32[]{:S(2)}) collective-permute-start(f32[136,128]{1,0:T(8,128)S(1)} %get-tuple-element.29), channel_id=1, source_target_pairs={{0,64},{1,129},{64,128},{65,193},{128,192},{129,65},{192,0},{193,1... | collective-permute-start | bytes 208904 | tf_op jit(solution)/shard_map/ppermute | solution.py:261
  33.5 0.7 %copy-start.3 = (f32[4,128]{1,0:T(4,128)S(1)}, f32[4,128]{1,0:T(4,128)}, u32[]{:S(2)}) copy-start(f32[4,128]{1,0:T(4,128)} %states.3) | copy-start | bytes 6148
  33.5 0.7 %copy-start.2 = (f32[4,64]{1,0:T(4,128)S(1)}, f32[4,64]{1,0:T(4,128)}, u32[]{:S(2)}) copy-start(f32[4,64]{1,0:T(4,128)} %controls.3) | copy-start | bytes 3076
  35.3 1.4 %copy-start.4 = (f32[128]{0:T(128)S(1)}, f32[128]{0:T(128)}, u32[]{:S(2)}) copy-start(f32[128]{0:T(128)} %param.15) | copy-start | bytes 1540
  35.3 2.5 %collective-permute-start.12 = (f32[8,128]{1,0:T(8,128)S(1)}, f32[8,128]{1,0:T(8,128)S(1)}, u32[]{:S(2)}, u32[]{:S(2)}) collective-permute-start(f32[8,128]{1,0:T(8,128)S(1)} %slice.35), channel_id=1, source_target_pairs={{0,192},{64,0},{128,64},{192,128},{1,193},{65,1},{129,65},{193,129... | collective-permute-start | bytes 12296 | tf_op jit(solution)/shard_map/ppermute | solution.py:210
  35.4 2.5 %collective-permute-start.11 = (f32[136,128]{1,0:T(8,128)S(1)}, f32[136,128]{1,0:T(8,128)S(1)}, u32[]{:S(2)}, u32[]{:S(2)}) collective-permute-start(f32[136,128]{1,0:T(8,128)S(1)} %collective-permute-done.10.own), channel_id=1, source_target_pairs={{0,1},{1,0},{2,3},{3,2},{4,5},{5,4},{6,7},{7,6},{8,9},{9,8},{10,11... | collective-permute-start | bytes 208904 | tf_op jit(solution)/shard_map/ppermute | solution.py:210
